TPU v7x, 32 devices: a whole 2x2x4 slice. The times are simulated.
32 devices in a mesh: groups: 2 (over x), blk: 8 (over z, y), head: 2 (over core).
Axes of the slice: x: 2, y: 2, z: 4, core: 2. Of those that a mesh axis runs over, the one named last changes fastest.
Arguments:
- queries: bfloat16 [1024, 36864], P(('groups', 'blk'), 'head'), parts along dimension 0, may hold values from -750 to 750
- latent_cache: bfloat16 [128, 576, 256], P(('groups', 'blk')), parts along dimension 0, may hold values from -6 to 6
- new_latent: bfloat16 [576, 1024], P(None, ('groups', 'blk')), parts along dimension 1, may hold values from -6 to 6
- span_len: int32 [16], P('groups'), parts along dimension 0, may hold values from 2 to 57, as said below
- dec_count: int32 [16], P('groups'), parts along dimension 0, may hold values from 1 to 7, as said below
- span_start: int32 [16], P(('groups', 'blk')), parts along dimension 0, may hold values from 0 to 256, as said below
- cache_len: int32 [16, 7], P(('groups', 'blk')), parts along dimension 0, may hold values from 2 to 256, as said below
- value_weight: bfloat16 [64, 512, 128], P('head'), may hold values from -0.25 to 0.25
- out_weight: bfloat16 [8192, 7168], P('head', 'blk'), may hold values from -0.0625 to 0.0625
- residual: bfloat16 [1024, 7168], P(('groups', 'blk')), parts along dimension 0, may hold values from -34 to 34
- norm_gain: float32 [7168], replicated, may hold values from 0.1 to 1.9
- gate_weight: bfloat16 [7168, 9216], P(None, ('blk', 'head')), may hold values from -0.0625 to 0.0625
- up_weight: bfloat16 [7168, 9216], P(None, ('blk', 'head')), may hold values from -0.0625 to 0.0625
- down_weight: bfloat16 [9216, 7168], P(('blk', 'head')), may hold values from -0.0625 to 0.0625
Outputs:
- mixed: bfloat16 [1024, 7168], P(('groups', 'blk', 'head')), parts along dimension 0
There are 2 independent parts, one for each index of `groups`. A program takes and returns all parts, laid end to end along the dimension named above; an argument that names none is the same for every part. Nothing has to cross between parts.
Inputs may be any that keep to these rules, and one draw needn't show every extreme that they name: span_len + dec_count is at most 64 on every rank, exactly 64 on one rank, at most 32 on every other rank and exactly 32 on some other rank; its sum over all ranks is exactly 256. `dec_count`: decode row j of a rank uses the rank's sequence slot j + 1. `span_start`: the cached positions of a rank's sequence slot 0. `cache_len`: entry j belongs to sequence slot j + 1; entries at or past a rank's dec_count are unused.
All inputs are finite; a program needn't handle non-finite values.
Results may differ from a plain program's by a relative error of at most 0.02.
Values may be sent and summed in bfloat16 or wider, within the bound.
A program may use at most 128 MiB of HBM per device.

v0:
```python
import jax
import jax.numpy as jnp
from jax import lax
from jax.sharding import PartitionSpec as P

score_scale = 192.0 ** (-0.5)
norm_eps = 1e-06
masked_score = -1e30


def rounded(values):
    return lax.optimization_barrier(values.astype(jnp.bfloat16)).astype(jnp.float32)


def pick_rank(values, rank_index):
    matches = jnp.arange(values.shape[0], dtype=jnp.int32) == rank_index
    return jnp.sum(jnp.where(matches, values, 0))


def local_attention(
    query_rows, cache_slots, fresh_keys, span_rows, decode_rows, start_pos, lengths, key_width
):
    row_count = query_rows.shape[0]
    slot_count = cache_slots.shape[0]
    positions = jnp.arange(cache_slots.shape[2], dtype=jnp.int32)
    local_rows = jnp.arange(row_count, dtype=jnp.int32)
    cached_scores = (
        jnp.einsum("rhl,lt->rht", query_rows, cache_slots[0], preferred_element_type=jnp.float32)
        * score_scale
    )
    fresh_scores = (
        jnp.einsum("rhl,lj->rhj", query_rows, fresh_keys, preferred_element_type=jnp.float32)
        * score_scale
    )
    cached_seen = (positions < start_pos)[None, None, :]
    fresh_seen = (local_rows[None, :] <= local_rows[:, None])[:, None, :]
    cached_scores = jnp.where(cached_seen, cached_scores, masked_score)
    fresh_scores = jnp.where(fresh_seen, fresh_scores, masked_score)
    peak_score = jnp.maximum(jnp.max(cached_scores, axis=2), jnp.max(fresh_scores, axis=2))[
        :, :, None
    ]
    cached_exp = jnp.where(cached_seen, jnp.exp(cached_scores - peak_score), 0.0)
    fresh_exp = jnp.where(fresh_seen, jnp.exp(fresh_scores - peak_score), 0.0)
    totals = jnp.sum(cached_exp, axis=2, keepdims=True) + jnp.sum(fresh_exp, axis=2, keepdims=True)
    span_out = jnp.einsum(
        "rht,lt->rhl",
        (cached_exp / totals).astype(jnp.bfloat16),
        cache_slots[0, :key_width],
        preferred_element_type=jnp.float32,
    )
    span_out = span_out + jnp.einsum(
        "rhj,lj->rhl",
        (fresh_exp / totals).astype(jnp.bfloat16),
        fresh_keys[:key_width],
        preferred_element_type=jnp.float32,
    )
    decode_slots = jnp.arange(slot_count - 1, dtype=jnp.int32)
    decode_index = jnp.clip(span_rows + decode_slots, 0, row_count - 1)
    decode_query = jnp.take(query_rows, decode_index, axis=0)
    decode_keys = cache_slots[1:]
    own_keys = jnp.take(fresh_keys, decode_index, axis=1)
    slot_scores = (
        jnp.einsum("shl,slt->sht", decode_query, decode_keys, preferred_element_type=jnp.float32)
        * score_scale
    )
    slot_seen = (positions[None, :] < lengths[:, None])[:, None, :]
    slot_scores = jnp.where(slot_seen, slot_scores, masked_score)
    own_scores = (
        jnp.einsum("shl,ls->sh", decode_query, own_keys, preferred_element_type=jnp.float32)
        * score_scale
    )
    slot_peak = jnp.maximum(jnp.max(slot_scores, axis=2), own_scores)
    slot_exp = jnp.where(slot_seen, jnp.exp(slot_scores - slot_peak[:, :, None]), 0.0)
    own_exp = jnp.exp(own_scores - slot_peak)
    slot_totals = jnp.sum(slot_exp, axis=2) + own_exp
    decode_out = jnp.einsum(
        "sht,slt->shl",
        (slot_exp / slot_totals[:, :, None]).astype(jnp.bfloat16),
        decode_keys[:, :key_width],
        preferred_element_type=jnp.float32,
    )
    decode_out = (
        decode_out
        + rounded(own_exp / slot_totals)[:, :, None]
        * own_keys[:key_width].T.astype(jnp.float32)[:, None, :]
    )
    placing = (
        (local_rows[:, None] == span_rows + decode_slots[None, :])
        & (decode_slots[None, :] < decode_rows)
    ).astype(jnp.float32)
    latent_out = jnp.where((local_rows < span_rows)[:, None, None], span_out, 0.0)
    latent_out = latent_out + jnp.einsum("is,shl->ihl", placing, decode_out)
    return latent_out.astype(jnp.bfloat16)


def padded_term(hidden, down_weight):
    return jnp.dot(hidden, down_weight, preferred_element_type=jnp.float32)


def on_device(
    queries,
    latent_cache,
    new_latent,
    span_len,
    dec_count,
    span_start,
    cache_len,
    value_weight,
    out_weight,
    residual,
    norm_gain,
    gate_weight,
    up_weight,
    down_weight,
):
    rank_index = lax.axis_index("blk")
    rows_dev = residual.shape[0]
    heads_here = value_weight.shape[0]
    lives = span_len + dec_count
    query_rows = queries.reshape(rows_dev, heads_here, queries.shape[1] // heads_here)
    latent_out = local_attention(
        query_rows,
        latent_cache,
        new_latent,
        pick_rank(span_len, rank_index),
        pick_rank(dec_count, rank_index),
        span_start[0],
        cache_len[0],
        value_weight.shape[1],
    )
    head_values = jnp.einsum(
        "rhl,hlv->rhv", latent_out, value_weight, preferred_element_type=jnp.float32
    )
    head_values = head_values.astype(jnp.bfloat16).reshape(
        rows_dev, heads_here * value_weight.shape[2]
    )
    partial_out = jnp.dot(
        lax.all_gather(head_values, "blk", axis=0, tiled=True),
        out_weight,
        preferred_element_type=jnp.float32,
    )
    summed_out = lax.psum(partial_out.astype(jnp.bfloat16), "head").astype(jnp.float32)
    attended = lax.all_to_all(
        summed_out.astype(jnp.bfloat16), "blk", split_axis=0, concat_axis=1, tiled=True
    ).astype(summed_out.dtype)
    stream = residual.astype(jnp.float32) + attended
    scale_rows = lax.rsqrt(jnp.mean(stream * stream, axis=1, keepdims=True) + norm_eps)
    normed = (stream * scale_rows * norm_gain[None, :]).astype(jnp.bfloat16)
    head_index = lax.axis_index("head")
    half_rows = rows_dev // lax.axis_size("head")
    row_piece = lax.all_gather(normed, "blk", axis=0, tiled=True)
    gate_values = jnp.dot(row_piece, gate_weight, preferred_element_type=jnp.float32)
    up_values = jnp.dot(row_piece, up_weight, preferred_element_type=jnp.float32)
    hidden = (jax.nn.silu(gate_values) * up_values).astype(jnp.bfloat16)
    projected = lax.psum_scatter(
        padded_term(hidden, down_weight).astype(jnp.bfloat16),
        ("blk", "head"),
        scatter_dimension=0,
        tiled=True,
    ).astype(jnp.float32)
    own_rows = head_index * half_rows + jnp.arange(half_rows, dtype=jnp.int32)
    alive = own_rows < pick_rank(lives, rank_index)
    stream_half = lax.dynamic_slice_in_dim(stream, head_index * half_rows, half_rows, 0)
    return jnp.where(alive[:, None], stream_half + projected, 0.0).astype(jnp.bfloat16)


def solution(mesh):
    placed = (
        P(("groups", "blk"), "head"),
        P(("groups", "blk"), None, None),
        P(None, ("groups", "blk")),
        P("groups"),
        P("groups"),
        P(("groups", "blk")),
        P(("groups", "blk"), None),
        P("head", None, None),
        P("head", "blk"),
        P(("groups", "blk"), None),
        P(),
        P(None, ("blk", "head")),
        P(None, ("blk", "head")),
        P(("blk", "head"), None),
    )
    return jax.shard_map(
        on_device,
        mesh=mesh,
        in_specs=placed,
        out_specs=P(("groups", "blk", "head"), None),
        check_vma=False,
    )
```

profile of v0, /device:TPU:0, one launch (start us, length us, event | category | flops | bytes accessed | tf_op | source)
XLA Modules:
  0.0 420.6 jit_solution(16827265597548043617)
XLA Ops:
  6.5 1.4 select_reduce_fusion.2
  10.3 4.5 %reshape.113 = bf16[64,32,576]{2,1,0:T(8,128)(2,1)S(1)} reshape(bf16[64,18432]{1,0:T(8,128)(2,1)} %param.14) | data formatting | bytes 4718592 | tf_op jit(solution)/shard_map/reshape | solution.py:120
  16.1 0.9 fusion.61
  17.7 1.1 fusion.2
  19.5 1.0 fusion.6
  20.5 0.8 divide_convert_fusion
  21.3 0.7 divide_convert_fusion.1
  22.0 1.3 compare_and_fusion
  24.5 2.9 fusion.20
  27.4 2.7 fusion.26
  30.7 6.3 %fusion.10 = bf16[32,8,8,128]{3,2,1,0:T(8,128)(2,1)S(1)} fusion(bf16[32,512,128]{2,1,0:T(8,128)(2,1)} %param.21, f32[64,32,512]{2,0,1:T(8,128)} %fusion.20, f32[64,32,512]{2,0,1:T(8,128)} %fusion.26, pred[64]{0:T(512)(128)(4,1)S(1)} %iota_compare_fusion.5, bf16[7,32,512]{2,1,0:T(8,128)(2,1)S(1)} %fusion.11, s32[7]{0:T(128)S(1)} %iota_add_fusion, ...), kind=kOutput, calls=%fused_computation.24 | convolution fusion | flops 287572864 | bytes 13336675 | tf_op jit(solution)/shard_map/rhl,hlv->rhv/dot_general | solution.py:131
  37.1 0.9 copy.50
  38.0 75.6 %all-gather.3.cloned.1.call-done = bf16[512,4096]{1,0:T(8,128)(2,1)} async-done(((bf16[64,4096]{1,0:T(8,128)(2,1)}), bf16[512,4096]{1,0:T(8,128)(2,1)}) %all-gather.3.cloned.1.call-update) | async-done | bytes 4194320 | tf_op jit(solution)/shard_map/all_gather | solution.py:138
  113.7 9.8 %convolution_convert_fusion.1 = bf16[512,896]{1,0:T(8,128)(2,1)} fusion(bf16[512,4096]{1,0:T(8,128)(2,1)} %all-gather.3.cloned.1.call-done, bf16[4096,896]{1,0:T(8,128)(2,1)} %param.22), kind=kOutput, calls=%fused_computation.18 | convolution fusion | flops 3758555136 | bytes 12451840 | tf_op jit(solution)/shard_map/dot_general | solution.py:137
  123.7 17.6 %all-reduce.2.cloned.1.call-done = bf16[8,64,896]{2,1,0:T(8,128)(2,1)} async-done(((bf16[8,64,896]{2,1,0:T(8,128)(2,1)}), bf16[8,64,896]{2,1,0:T(8,128)(2,1)}) %all-reduce.2.cloned.1.call-update) | async-done | bytes 917520 | tf_op jit(solution)/shard_map/psum | solution.py:142
  141.3 29.5 %all_to_all.13 = bf16[8,64,896]{2,1,0:T(8,128)(2,1)S(1)} all-to-all(bf16[8,64,896]{2,1,0:T(8,128)(2,1)} %all-reduce.2.cloned.1.call-done), channel_id=1, replica_groups=mesh['groups'=2,'blk'=8,'head'=2] {'blk'}, dimensions={0} | all-to-all | bytes 1835008 | tf_op jit(solution)/shard_map/all_to_all | solution.py:143
  171.2 1.0 copy-done.3
  172.5 1.2 copy-done.1
  173.8 1.2 multiply_convert_fusion
  175.0 110.2 %all-gather.5.cloned.1.call-done = bf16[512,7168]{1,0:T(8,128)(2,1)} async-done(((bf16[64,7168]{1,0:T(8,128)(2,1)}), bf16[512,7168]{1,0:T(8,128)(2,1)}) %all-gather.5.cloned.1.call-update) | async-done | bytes 7340048 | tf_op jit(solution)/shard_map/all_gather | solution.py:151
  285.3 9.0 %fusion.63 = f32[512,576]{0,1:T(8,128)S(1)} fusion(bf16[512,7168]{1,0:T(8,128)(2,1)} %all-gather.5.cloned.1.call-done, bf16[7168,576]{0,1:T(8,128)(2,1)} %param.25), kind=kOutput, calls=%fused_computation.95 | convolution fusion | flops 4227858432 | bytes 16777216 | tf_op jit(solution)/shard_map/dot_general | solution.py:152
  294.3 27.8 %convolution_convert_fusion = bf16[512,7168]{1,0:T(8,128)(2,1)} fusion(bf16[576,7168]{1,0:T(8,128)(2,1)} %param.27, bf16[512,7168]{1,0:T(8,128)(2,1)} %all-gather.5.cloned.1.call-done, bf16[7168,576]{0,1:T(8,128)(2,1)} %param.26, f32[512,576]{0,1:T(8,128)S(1)} %fusion.63), kind=kOutput, calls=%fused_computation.2 | convolution fusion | flops 8461156352 | bytes 32374784 | tf_op jit(solution)/shard_map/dot_general | solution.py:97
  322.8 89.3 %reduce-scatter.2.cloned.1.call-done = bf16[32,7168]{1,0:T(8,128)(2,1)} async-done(((bf16[512,7168]{1,0:T(8,128)(2,1)}), bf16[32,7168]{1,0:T(8,128)(2,1)}) %reduce-scatter.2.cloned.1.call-update) | async-done | bytes 458768 | tf_op jit(solution)/shard_map/reduce_scatter | solution.py:155
  412.1 1.9 select_convert_fusion
  (46 shorter events, 7.8 us)
Async XLA Ops:
  6.5 107.1 %all-gather.3.cloned.1.call-start = ((), (), s32[]{:S(2)}) async-start(), calls=%async_computation.2 | async-start | bytes 4718592 | tf_op jit(solution)/shard_map/all_gather | solution.py:138
  10.3 4.5 %copy-start = (bf16[576,64]{0,1:T(8,128)(2,1)S(1)}, bf16[576,64]{0,1:T(8,128)(2,1)}, u32[]{:S(2)}) copy-start(bf16[576,64]{0,1:T(8,128)(2,1)} %param.16) | copy-start | bytes 221188
  16.1 1.7 copy-start.4
  20.5 2.8 copy-start.6
  38.0 103.4 %all-reduce.2.cloned.1.call-start = ((), (), s32[]{:S(2)}) async-start(), calls=%async_computation.3 | async-start | bytes 1835008 | tf_op jit(solution)/shard_map/psum | solution.py:142
  123.5 161.8 %all-gather.5.cloned.1.call-start = ((), (), s32[]{:S(2)}) async-start(), calls=%async_computation.4 | async-start | bytes 8257536 | tf_op jit(solution)/shard_map/all_gather | solution.py:151
  171.0 1.2 copy-start.3
  171.1 2.6 copy-start.5
  172.5 1.3 copy-start.1
  175.0 237.2 %reduce-scatter.2.cloned.1.call-start = ((), (), s32[]{:S(2)}) async-start(), calls=%async_computation.5 | async-start | bytes 7798784 | tf_op jit(solution)/shard_map/reduce_scatter | solution.py:155
  322.1 90.0 %copy-start.2 = (f32[64,7168]{1,0:T(8,128)S(1)}, f32[64,7168]{1,0:T(8,128)}, u32[]{:S(2)}) copy-start(f32[64,7168]{1,0:T(8,128)} %copy-done.1) | copy-start | bytes 5505028
Sparse Core Ops, SparseCore 0:
  38.1 75.5 all-gather.2
  123.6 17.6 all-reduce.1
  175.1 110.1 all-gather.4
  322.3 89.8 reduce-scatter.1
where the time goes:
time: 421 us
  waiting for transfers between devices  293 us (70%)
  matrix products  62 us (15%)
  blocking collectives  29.5 us (7%)
  between operations  14 us (3%)
  other arithmetic  12.1 us (3%)
  local copies, waits for them, and re-layouts  9.72 us (2%)
    all_gather x1, waiting for transfers between devices, on_device(): row_piece = lax.all_gather(normed, 'blk', axis=0, tiled=True)  110 us
    reduce_scatter x1, waiting for transfers between devices, on_device(): lax.psum_scatter(padded_term(hidden, down_weight).astype(jnp.bfloat16), (...  89.3 us
    all_gather x1, waiting for transfers between devices, on_device(): lax.all_gather(head_values, 'blk', axis=0, tiled=True)  75.6 us
    all_to_all x1, blocking collectives, on_device(): lax.all_to_all(summed_out.astype(jnp.bfloat16), 'blk', split_axis=0, conc...  29.5 us
    dot_general x1, matrix products, padded_term(): return jnp.dot(hidden, down_weight, preferred_element_type=jnp.float32)  27.8 us
    psum x1, waiting for transfers between devices, on_device(): lax.psum(partial_out.astype(jnp.bfloat16), 'head').astype(jnp.float32)  17.6 us
    dot_general x1, matrix products, on_device(): jnp.dot(lax.all_gather(head_values, 'blk', axis=0, tiled=True), out_weigh...  9.78 us
    dot_general x1, matrix products, on_device(): jnp.dot(row_piece, gate_weight, preferred_element_type=jnp.float32)  9.02 us
  transfers between devices with their start and end apart: 4, of which 4 were waited for; matrix products, arithmetic and copies ran while one was open for 0% of the time, Pallas kernels for 0%

commit v1 on v0

--- a/solution.py
+++ b/solution.py
@@ -91,10 +91,6 @@
     latent_out = jnp.where((local_rows < span_rows)[:, None, None], span_out, 0.0)
     latent_out = latent_out + jnp.einsum("is,shl->ihl", placing, decode_out)
     return latent_out.astype(jnp.bfloat16)
-
-
-def padded_term(hidden, down_weight):
-    return jnp.dot(hidden, down_weight, preferred_element_type=jnp.float32)
 
 
 def on_device(
@@ -134,33 +130,56 @@
     head_values = head_values.astype(jnp.bfloat16).reshape(
         rows_dev, heads_here * value_weight.shape[2]
     )
-    partial_out = jnp.dot(
-        lax.all_gather(head_values, "blk", axis=0, tiled=True),
-        out_weight,
-        preferred_element_type=jnp.float32,
-    )
-    summed_out = lax.psum(partial_out.astype(jnp.bfloat16), "head").astype(jnp.float32)
-    attended = lax.all_to_all(
-        summed_out.astype(jnp.bfloat16), "blk", split_axis=0, concat_axis=1, tiled=True
-    ).astype(summed_out.dtype)
-    stream = residual.astype(jnp.float32) + attended
-    scale_rows = lax.rsqrt(jnp.mean(stream * stream, axis=1, keepdims=True) + norm_eps)
-    normed = (stream * scale_rows * norm_gain[None, :]).astype(jnp.bfloat16)
+    first = rows_dev // 2
+    is_full = pick_rank(lives, rank_index) > first
+    width = out_weight.shape[1]
+    ranks = lax.axis_size("blk")
+    moved = lax.all_to_all(
+        residual.reshape(rows_dev, ranks, width).transpose(1, 0, 2),
+        "blk",
+        split_axis=0,
+        concat_axis=0,
+        tiled=True,
+    )
+    full_ranks = (lives > first)[:, None, None]
+    residual_rows = jnp.concatenate(
+        [
+            moved[:, :first].reshape(ranks * first, width).astype(jnp.float32),
+            jnp.sum(jnp.where(full_ranks, moved[:, first:], 0).astype(jnp.float32), axis=0),
+        ]
+    )
+    rest = jnp.where(is_full, head_values[first:], 0).astype(jnp.bfloat16)
+    packed = jnp.concatenate(
+        [
+            lax.all_gather(head_values[:first], "blk", axis=0, tiled=True),
+            lax.psum(rest, "blk"),
+        ]
+    )
+    partial_out = jnp.dot(packed, out_weight, preferred_element_type=jnp.float32)
+    attended = lax.psum(partial_out.astype(jnp.bfloat16), "head").astype(jnp.float32)
+    stream = lax.all_gather(
+        (residual_rows + attended).astype(jnp.bfloat16), "blk", axis=1, tiled=True
+    )
+    wide = stream.astype(jnp.float32)
+    scale_rows = lax.rsqrt(jnp.mean(wide * wide, axis=1, keepdims=True) + norm_eps)
+    normed = (wide * scale_rows * norm_gain[None, :]).astype(jnp.bfloat16)
+    gate_values = jnp.dot(normed, gate_weight, preferred_element_type=jnp.float32)
+    up_values = jnp.dot(normed, up_weight, preferred_element_type=jnp.float32)
+    hidden = (jax.nn.silu(gate_values) * up_values).astype(jnp.bfloat16)
+    partial = jnp.dot(hidden, down_weight, preferred_element_type=jnp.float32).astype(jnp.bfloat16)
     head_index = lax.axis_index("head")
-    half_rows = rows_dev // lax.axis_size("head")
-    row_piece = lax.all_gather(normed, "blk", axis=0, tiled=True)
-    gate_values = jnp.dot(row_piece, gate_weight, preferred_element_type=jnp.float32)
-    up_values = jnp.dot(row_piece, up_weight, preferred_element_type=jnp.float32)
-    hidden = (jax.nn.silu(gate_values) * up_values).astype(jnp.bfloat16)
-    projected = lax.psum_scatter(
-        padded_term(hidden, down_weight).astype(jnp.bfloat16),
-        ("blk", "head"),
-        scatter_dimension=0,
+    owned = lax.all_gather(
+        lax.psum_scatter(partial[: ranks * first], ("blk", "head"), scatter_dimension=0, tiled=True),
+        "head",
+        axis=0,
         tiled=True,
-    ).astype(jnp.float32)
-    own_rows = head_index * half_rows + jnp.arange(half_rows, dtype=jnp.int32)
+    )
+    spare = lax.psum(partial[ranks * first :], ("blk", "head"))
+    projected = jnp.where(head_index == 0, owned, spare).astype(jnp.float32)
+    place = jnp.where(head_index == 0, rank_index, ranks) * first
+    stream_half = lax.dynamic_slice_in_dim(stream, place, first, 0).astype(jnp.float32)
+    own_rows = head_index * first + jnp.arange(first, dtype=jnp.int32)
     alive = own_rows < pick_rank(lives, rank_index)
-    stream_half = lax.dynamic_slice_in_dim(stream, head_index * half_rows, half_rows, 0)
     return jnp.where(alive[:, None], stream_half + projected, 0.0).astype(jnp.bfloat16)
 
 

time: 421 us -> 471 us (1.12)
  waiting for transfers between devices: 293 us -> 366 us
  blocking collectives: 29.5 us -> 2.33 us
  matrix products: 62 us -> 48.7 us
  starting transfers between devices: 0.31 us -> 7.7 us
  local copies, waits for them, and re-layouts: 9.72 us -> 14.5 us
    psum x0 -> x2, waiting for transfers between devices: none -> 160 us  [the longest x1 90.4 us: on_device(): spare = lax.psum(partial[ranks * first:], ('blk', 'head'))]
    all_gather x2, waiting for transfers between devices: 186 us -> 124 us  [the longest x1 73.2 us: on_device(): lax.all_gather((residual_rows + attended).astype(jnp.bfloat16), 'blk', ax...]
    all_to_all x1 -> x0, blocking collectives: 29.5 us -> none  [on_device(): lax.all_to_all(summed_out.astype(jnp.bfloat16), 'blk', split_axis=0, conc...]
    reduce_scatter x1, waiting for transfers between devices: 89.3 us -> 64.6 us  [on_device(): lax.psum_scatter(partial[:ranks * first], ('blk', 'head'), scatter_dimens...]
    dot_general x3, matrix products: 46.6 us -> 30.8 us  [the longest x1 17.6 us: on_device(): jnp.dot(hidden, down_weight, preferred_element_type=jnp.float32)]
    all_to_all x0 -> x1, starting transfers between devices: none -> 7.31 us  [on_device(): lax.all_to_all(residual.reshape(rows_dev, ranks, width).transpose(1, 0, 2...]
    slice x0 -> x4, local copies, waits for them, and re-layouts: none -> 6.79 us  [the longest x1 4.17 us: on_device(): partial[:ranks * first]]
  transfers between devices with their start and end apart: 4 -> 7, of which waited for: 4 -> 6; matrix products, arithmetic and copies ran while one was open for 0% -> 3% of each run, Pallas kernels for 0% -> 0%
where the time goes in v1:
time: 471 us; the launch traced here: 470 us
  waiting for transfers between devices  366 us (78%)
  matrix products  48.7 us (10%)
  other arithmetic  16 us (3%)
  between operations  15.1 us (3%)
  local copies, waits for them, and re-layouts  14.5 us (3%)
  starting transfers between devices  7.7 us (2%)
    psum x1, waiting for transfers between devices, on_device(): spare = lax.psum(partial[ranks * first:], ('blk', 'head'))  90.4 us
    all_gather x1, waiting for transfers between devices, on_device(): lax.all_gather((residual_rows + attended).astype(jnp.bfloat16), 'blk', ax...  73.2 us
    psum x1, waiting for transfers between devices, on_device(): lax.psum(rest, 'blk')  70.1 us
    reduce_scatter x1, waiting for transfers between devices, on_device(): lax.psum_scatter(partial[:ranks * first], ('blk', 'head'), scatter_dimens...  64.6 us
    all_gather x1, waiting for transfers between devices, on_device(): lax.all_gather(head_values[:first], 'blk', axis=0, tiled=True)  50.5 us
    dot_general x1, matrix products, on_device(): jnp.dot(hidden, down_weight, preferred_element_type=jnp.float32)  17.6 us
    psum x1, waiting for transfers between devices, on_device(): lax.psum(partial_out.astype(jnp.bfloat16), 'head').astype(jnp.float32)  16.9 us
  transfers between devices with their start and end apart: 7, of which 6 were waited for; matrix products, arithmetic and copies ran while one was open for 3% of the time, Pallas kernels for 0%

profile of v1, /device:TPU:0, one launch (start us, length us, event | category | flops | bytes accessed | tf_op | source)
XLA Modules:
  0.0 470.0 jit_solution(13670419200864394861)
XLA Ops:
  6.6 1.4 select_reduce_fusion.2
  8.6 4.5 reshape.119
  15.9 2.1 fusion.9
  22.2 1.3 compare_and_fusion
  24.8 2.7 fusion.39
  27.4 2.9 fusion.33
  31.0 2.1 fusion.21
  33.2 6.4 %fusion.20 = bf16[64,32,128]{2,0,1:T(8,128)(2,1)S(1)} fusion(bf16[32,512,128]{2,1,0:T(8,128)(2,1)} %param.21, f32[64,32,512]{2,0,1:T(8,128)} %fusion.33, f32[64,32,512]{2,0,1:T(8,128)} %fusion.39, pred[64]{0:T(512)(128)(4,1)S(1)} %iota_compare_fusion.5, bf16[7,32,512]{2,1,0:T(8,128)(2,1)S(1)} %fusion.21, s32[7]{0:T(128)S(1)} %iota_add_fusion, ...), kind=kOutput, calls=%fused_computation.29 | convolution fusion | flops 287572864 | bytes 13336675 | tf_op jit(solution)/shard_map/rhl,hlv->rhv/dot_general | solution.py:127
  42.3 7.3 %all-to-all-start = ((bf16[8,64,896]{2,1,0:T(8,128)(2,1)}), bf16[8,64,896]{2,1,0:T(8,128)(2,1)S(1)}, u32[]{:S(2)}, u32[]{:S(2)}) async-start(bf16[8,64,896]{2,1,0:T(8,128)(2,1)} %bitcast.80), calls=%async_computation | async-start | bytes 1835008 | tf_op jit(solution)/shard_map/all_to_all | solution.py:137
  49.7 70.1 %all-reduce.4.cloned.1.call-done = bf16[32,4096]{1,0:T(8,128)(2,1)} async-done(((bf16[32,4096]{1,0:T(8,128)(2,1)}), bf16[32,4096]{1,0:T(8,128)(2,1)}) %all-reduce.4.cloned.1.call-update) | async-done | bytes 262160 | tf_op jit(solution)/shard_map/psum | solution.py:155
  119.7 50.5 %all-gather.3.cloned.1.call-done = bf16[256,4096]{1,0:T(8,128)(2,1)} async-done(((bf16[32,4096]{1,0:T(8,128)(2,1)}), bf16[256,4096]{1,0:T(8,128)(2,1)}) %all-gather.3.cloned.1.call-update) | async-done | bytes 2097168 | tf_op jit(solution)/shard_map/all_gather | solution.py:154
  170.2 7.2 %fusion.16 = bf16[288,896]{1,0:T(8,128)(2,1)} fusion(bf16[4096,896]{1,0:T(8,128)(2,1)} %param.22, bf16[32,4096]{1,0:T(8,128)(2,1)} %all-reduce.4.cloned.1.call-done, bf16[256,4096]{1,0:T(8,128)(2,1)} %all-gather.3.cloned.1.call-done), kind=kOutput, calls=%fused_computation.26 | convolution fusion | flops 2118905856 | bytes 10215424 | tf_op jit(solution)/shard_map/dot_general | solution.py:158
  177.8 16.9 %all-reduce.6.cloned.1.call-done = bf16[288,896]{1,0:T(8,128)(2,1)} async-done(((bf16[288,896]{1,0:T(8,128)(2,1)}), bf16[288,896]{1,0:T(8,128)(2,1)}) %all-reduce.6.cloned.1.call-update) | async-done | bytes 516112 | tf_op jit(solution)/shard_map/psum | solution.py:159
  194.7 1.9 fusion.35
  196.9 73.2 %all-gather.5.cloned.1.call-done = bf16[288,7168]{1,0:T(8,128)(2,1)} async-done(((bf16[288,896]{1,0:T(8,128)(2,1)}), bf16[288,7168]{1,0:T(8,128)(2,1)}) %all-gather.5.cloned.1.call-update) | async-done | bytes 4128784 | tf_op jit(solution)/shard_map/all_gather | solution.py:160
  270.0 3.2 fusion
  273.4 5.9 %fusion.25 = f32[288,576]{1,0:T(8,128)S(1)} fusion(bf16[7168,576]{0,1:T(8,128)(2,1)} %param.25, bf16[288,7168]{1,0:T(8,128)(2,1)S(1)} %copy-done.1, f32[7168]{0:T(1024)S(1)} %copy-done.7, f32[288]{0:T(512)S(1)} %add_rsqrt_fusion), kind=kOutput, calls=%fused_computation.31 | convolution fusion | flops 2386427904 | bytes 13079680 | tf_op jit(solution)/shard_map/dot_general | solution.py:166
  279.4 17.6 %convolution_convert_fusion = bf16[288,7168]{1,0:T(8,128)(2,1)} fusion(bf16[576,7168]{1,0:T(8,128)(2,1)} %param.27, bf16[7168,576]{0,1:T(8,128)(2,1)} %param.26, bf16[288,7168]{1,0:T(8,128)(2,1)} %all-gather.5.cloned.1.call-done, f32[7168]{0:T(1024)S(1)} %copy-done.7, f32[288]{0:T(512)S(1)} %add_rsqrt_fusion, f32[288,576]{1,0:T(8,128)S(1)} %fusion.25), kind=kOutput, calls=%fused_computation.4 | convolution fusion | flops 4767657984 | bytes 25465984 | tf_op jit(solution)/shard_map/dot_general | solution.py:169
  297.0 4.2 slice.63
  301.3 1.8 slice.64
  303.8 64.6 %reduce-scatter.2.cloned.1.call-done = bf16[16,7168]{1,0:T(8,128)(2,1)} async-done(((bf16[256,7168]{1,0:T(8,128)(2,1)}), bf16[16,7168]{1,0:T(8,128)(2,1)}) %reduce-scatter.2.cloned.1.call-update) | async-done | bytes 229392 | tf_op jit(solution)/shard_map/reduce_scatter | solution.py:172
  368.4 2.3 all_gather.11
  370.8 90.4 %all-reduce.8.cloned.1.call-done = bf16[32,7168]{1,0:T(8,128)(2,1)} async-done(((bf16[32,7168]{1,0:T(8,128)(2,1)}), bf16[32,7168]{1,0:T(8,128)(2,1)}) %all-reduce.8.cloned.1.call-update) | async-done | bytes 458768 | tf_op jit(solution)/shard_map/psum | solution.py:177
  461.2 2.0 select_convert_fusion
  (63 shorter events, 12.5 us)
Async XLA Ops:
  6.5 6.5 %copy-start = (bf16[576,64]{0,1:T(8,128)(2,1)S(1)}, bf16[576,64]{0,1:T(8,128)(2,1)}, u32[]{:S(2)}) copy-start(bf16[576,64]{0,1:T(8,128)(2,1)} %param.16) | copy-start | bytes 221188
  6.5 113.2 %all-reduce.4.cloned.1.call-start = ((), (), s32[]{:S(2)}) async-start(), calls=%async_computation.3 | async-start | bytes 524288 | tf_op jit(solution)/shard_map/psum | solution.py:155
  17.9 5.6 %copy-start.4 = (s32[1,7]{1,0:T(1,128)S(1)}, s32[1,7]{1,0:T(1,128)}, u32[]{:S(2)}) copy-start(s32[1,7]{1,0:T(1,128)} %param.20) | copy-start | bytes 88
  18.6 5.3 %copy-start.3 = (bf16[8,576,256]{2,1,0:T(8,128)(2,1)S(1)}, bf16[8,576,256]{2,1,0:T(8,128)(2,1)}, u32[]{:S(2)}) copy-start(bf16[8,576,256]{2,1,0:T(8,128)(2,1)} %param.15) | copy-start | bytes 7077892
  33.2 8.1 %copy-start.2 = (bf16[64,7168]{1,0:T(8,128)(2,1)S(1)}, bf16[64,7168]{1,0:T(8,128)(2,1)}, u32[]{:S(2)}) copy-start(bf16[64,7168]{1,0:T(8,128)(2,1)} %param.23) | copy-start | bytes 2752516
  40.4 129.8 %all-gather.3.cloned.1.call-start = ((), (), s32[]{:S(2)}) async-start(), calls=%async_computation.2 | async-start | bytes 2359296 | tf_op jit(solution)/shard_map/all_gather | solution.py:154
  42.3 135.2 %all-to-all-start = ((bf16[8,64,896]{2,1,0:T(8,128)(2,1)}), bf16[8,64,896]{2,1,0:T(8,128)(2,1)S(1)}, u32[]{:S(2)}, u32[]{:S(2)}) async-start(bf16[8,64,896]{2,1,0:T(8,128)(2,1)} %bitcast.80), calls=%async_computation | async-start | bytes 1835008 | tf_op jit(solution)/shard_map/all_to_all | solution.py:137
  49.6 127.9 %copy-start.5 = (s32[8]{0:T(128)S(1)}, s32[8]{0:T(128)}, u32[]{:S(2)}) copy-start(s32[8]{0:T(128)} %param.17) | copy-start | bytes 100
  49.6 127.9 %copy-start.6 = (s32[8]{0:T(128)S(1)}, s32[8]{0:T(128)}, u32[]{:S(2)}) copy-start(s32[8]{0:T(128)} %param.18) | copy-start | bytes 100
  49.6 145.1 %all-reduce.6.cloned.1.call-start = ((), (), s32[]{:S(2)}) async-start(), calls=%async_computation.4 | async-start | bytes 1032192 | tf_op jit(solution)/shard_map/psum | solution.py:159
  177.4 92.6 %all-gather.5.cloned.1.call-start = ((), (), s32[]{:S(2)}) async-start(), calls=%async_computation.5 | async-start | bytes 4644864 | tf_op jit(solution)/shard_map/all_gather | solution.py:160
  177.7 95.5 %copy-start.7 = (f32[7168]{0:T(1024)S(1)}, f32[7168]{0:T(1024)}, u32[]{:S(2)}) copy-start(f32[7168]{0:T(1024)} %param.24) | copy-start | bytes 86020
  196.6 171.8 %reduce-scatter.2.cloned.1.call-start = ((), (), s32[]{:S(2)}) async-start(), calls=%async_computation.6 | async-start | bytes 3899392 | tf_op jit(solution)/shard_map/reduce_scatter | solution.py:172
  270.0 3.4 copy-start.1
  301.2 160.0 %all-reduce.8.cloned.1.call-start = ((), (), s32[]{:S(2)}) async-start(), calls=%async_computation.7 | async-start | bytes 917504 | tf_op jit(solution)/shard_map/psum | solution.py:177
Sparse Core Ops, SparseCore 0:
  40.5 79.1 all-reduce.3
  121.9 48.2 all-gather.2
  177.5 17.1 all-reduce.5
  196.8 73.2 all-gather.4
  301.3 67.0 reduce-scatter.1
  371.7 89.4 all-reduce.7

commit v2 on v1

--- a/solution.py
+++ b/solution.py
@@ -1,7 +1,10 @@
 import jax
 import jax.numpy as jnp
 from jax import lax
+from jax.experimental import pallas as pl
+from jax.experimental.pallas import tpu as pltpu
 from jax.sharding import PartitionSpec as P
+import functools
 
 score_scale = 192.0 ** (-0.5)
 norm_eps = 1e-06
@@ -91,6 +94,398 @@
     latent_out = jnp.where((local_rows < span_rows)[:, None, None], span_out, 0.0)
     latent_out = latent_out + jnp.einsum("is,shl->ihl", placing, decode_out)
     return latent_out.astype(jnp.bfloat16)
+
+
+def send(src, dst, sent, landed, **device):
+    return pltpu.make_async_remote_copy(
+        src_ref=src,
+        dst_ref=dst,
+        send_sem=sent,
+        recv_sem=landed,
+        device_id=device,
+        device_id_type=pl.DeviceIdType.MESH,
+    )
+
+
+class Line:
+    def __init__(self, ranks):
+        self.rank = lax.axis_index("blk")
+        self.head = lax.axis_index("head")
+        self.count = ranks // 2
+        self.z = lax.div(self.rank, 2)
+        self.y = lax.rem(self.rank, 2)
+        self.has_up = self.z < self.count - 1
+        self.has_down = self.z > 0
+        self.up = self.rank + 2
+        self.down = self.rank - 2
+        self.across = self.rank + 1 - 2 * self.y
+        self.twin = 1 - self.head
+
+    def greet(self, with_twin):
+        barrier = pltpu.get_barrier_semaphore()
+
+        def signal(**device):
+            pl.semaphore_signal(
+                barrier, inc=1, device_id=device, device_id_type=pl.DeviceIdType.MESH
+            )
+
+        signal(blk=self.across)
+        if with_twin:
+            signal(head=self.twin)
+        pl.when(self.has_up)(lambda: signal(blk=self.up))
+        pl.when(self.has_down)(lambda: signal(blk=self.down))
+        ends = (self.z == 0).astype(jnp.int32) + (self.z == self.count - 1).astype(jnp.int32)
+        pl.semaphore_wait(barrier, (4 if with_twin else 3) - ends)
+
+
+def gather_ranks(line, own, place, up_sem, down_sem, across_sem, landed, arrived, between):
+    def to_up(s, src):
+        slot = 2 * s + line.y
+        return send(src, place(slot), up_sem.at[s], landed.at[slot], blk=line.up)
+
+    def to_down(s, src):
+        slot = 2 * s + line.y
+        return send(src, place(slot), down_sem.at[s], landed.at[slot], blk=line.down)
+
+    def to_across(s, src):
+        slot = 2 * s + line.y
+        return send(src, place(slot), across_sem.at[s], landed.at[slot], blk=line.across)
+
+    pl.when(line.has_up)(lambda: to_up(line.z, own).start())
+    pl.when(line.has_down)(lambda: to_down(line.z, own).start())
+    to_across(line.z, own).start()
+    for step in range(1, line.count):
+        low, high = line.z - step, line.z + step
+
+        @pl.when(low >= 0)
+        def _():
+            held = place(2 * low + line.y)
+            to_up(low, held).wait_recv()
+            pl.when(line.has_up)(lambda: to_up(low, held).start())
+            to_across(low, held).start()
+            arrived(2 * low + line.y)
+
+        @pl.when(high < line.count)
+        def _():
+            held = place(2 * high + line.y)
+            to_down(high, held).wait_recv()
+            pl.when(line.has_down)(lambda: to_down(high, held).start())
+            to_across(high, held).start()
+            arrived(2 * high + line.y)
+
+        between(step)
+    for s in range(line.count):
+        slot = 2 * s + 1 - line.y
+        send(place(slot), place(slot), across_sem.at[s], landed.at[slot], blk=line.across).wait_recv()
+        arrived(slot)
+    for s in range(line.count):
+        held = place(2 * s + line.y)
+        to_across(s, held).wait_send()
+        pl.when(line.has_up & (s <= line.z))(lambda: to_up(s, held).wait_send())
+        pl.when(line.has_down & (s >= line.z))(lambda: to_down(s, held).wait_send())
+
+
+class LineSum:
+    def __init__(self, line, own, work, sent, landed):
+        self.line, self.own, self.work, self.sent, self.landed = line, own, work, sent, landed
+
+    def copy(self, src, kind, **device):
+        return send(
+            self.work.at[src], self.work.at[kind], self.sent.at[kind], self.landed.at[kind], **device
+        )
+
+    def step(self, index):
+        line = self.line
+
+        @pl.when(line.z == index)
+        def _():
+            self.work[3] = self.own()
+            if index > 0:
+                self.copy(3, 0, blk=line.up).wait_recv()
+                self.work[3] = self.work[3] + self.work[0]
+            pl.when(line.has_up)(lambda: self.copy(3, 0, blk=line.up).start())
+
+        @pl.when(line.z == line.count - 1 - index)
+        def _():
+            self.work[4] = self.own()
+            if index > 0:
+                self.copy(4, 1, blk=line.down).wait_recv()
+                self.work[4] = self.work[4] + self.work[1]
+            pl.when(line.has_down)(lambda: self.copy(4, 1, blk=line.down).start())
+
+    def column(self):
+        self.work[5] = (
+            self.work[3].astype(jnp.float32)
+            + self.work[4].astype(jnp.float32)
+            - self.own().astype(jnp.float32)
+        ).astype(self.work.dtype)
+
+    def across(self):
+        return self.copy(5, 2, blk=self.line.across)
+
+    def total(self):
+        self.across().wait_recv()
+        return self.work[5].astype(jnp.float32) + self.work[2].astype(jnp.float32)
+
+    def drain(self):
+        line = self.line
+        self.across().wait_send()
+        pl.when(line.has_up)(lambda: self.copy(3, 0, blk=line.up).wait_send())
+        pl.when(line.has_down)(lambda: self.copy(4, 1, blk=line.down).wait_send())
+
+
+def rows_kernel(ranks, own, rest, out, work, up_sem, down_sem, across_sem, landed, sum_sent, sum_landed):
+    line = Line(ranks)
+    line.greet(False)
+    sums = LineSum(line, lambda: rest[...], work, sum_sent, sum_landed)
+    sums.step(0)
+    out[:, line.rank] = own[...]
+
+    def between(step):
+        sums.step(step)
+        if step == line.count - 1:
+            sums.column()
+            sums.across().start()
+
+    gather_ranks(
+        line, own, lambda slot: out.at[:, slot], up_sem, down_sem, across_sem, landed,
+        lambda slot: None, between,
+    )
+    out[:, ranks] = sums.total().astype(out.dtype)
+    sums.drain()
+
+
+def gather_rows(own, rest, ranks):
+    halves, rows, width = own.shape
+    count = ranks // 2
+    dma = pltpu.SemaphoreType.DMA
+    return pl.pallas_call(
+        functools.partial(rows_kernel, ranks),
+        out_shape=jax.ShapeDtypeStruct((halves, ranks + 1, rows, width), own.dtype),
+        in_specs=[pl.BlockSpec(memory_space=pltpu.VMEM)] * 2,
+        out_specs=pl.BlockSpec(memory_space=pltpu.VMEM),
+        scratch_shapes=[
+            pltpu.VMEM((6, halves, rows, width), own.dtype),
+            dma((count,)), dma((count,)), dma((count,)), dma((ranks,)), dma((3,)), dma((3,)),
+        ],
+        compiler_params=pltpu.CompilerParams(
+            collective_id=0, has_side_effects=True, vmem_limit_bytes=40 * 2**20
+        ),
+        name="gather_rows",
+    )(own, rest)
+
+
+def stream_kernel(
+    ranks, partial, residual, out, other, mine, up_sem, down_sem, across_sem, landed, pair_sem, twin_sent, twin_landed
+):
+    line = Line(ranks)
+    line.greet(True)
+    rows, width = mine.shape
+    pair = send(partial.at[line.twin], other, pair_sem.at[0], pair_sem.at[1], head=line.twin)
+    pair.start()
+    pair.wait_recv()
+    mine[...] = (
+        residual[line.head].astype(jnp.float32)
+        + partial[line.head].astype(jnp.float32)
+        + other[...].astype(jnp.float32)
+    ).astype(mine.dtype)
+
+    def spot(head, slot):
+        if len(out.shape) == 4:
+            return head, slot
+        return (
+            pl.ds(pl.multiple_of(head * rows, rows), rows),
+            pl.ds(pl.multiple_of(slot * width, width), width),
+        )
+
+    def place(head, slot):
+        return out.at[spot(head, slot)]
+
+    def to_twin(slot, src):
+        return send(
+            src, place(line.head, slot), twin_sent.at[slot], twin_landed.at[slot], head=line.twin
+        )
+
+    def arrived(slot):
+        to_twin(slot, place(line.head, slot)).start()
+
+    to_twin(line.rank, mine).start()
+    out[spot(line.head, line.rank)] = mine[...]
+    gather_ranks(
+        line, mine, lambda slot: place(line.head, slot), up_sem, down_sem, across_sem, landed,
+        arrived, lambda step: None,
+    )
+    for slot in range(ranks):
+        send(
+            mine, place(line.twin, slot), twin_sent.at[slot], twin_landed.at[slot], head=line.twin
+        ).wait_recv()
+        to_twin(slot, mine).wait_send()
+    pair.wait_send()
+
+
+def gather_stream(partial, residual, ranks):
+    halves, rows, width = partial.shape
+    count = ranks // 2
+    dma = pltpu.SemaphoreType.DMA
+    joined = width % 128 == 0
+    shape = (halves * rows, ranks * width) if joined else (halves, ranks, rows, width)
+    stream = pl.pallas_call(
+        functools.partial(stream_kernel, ranks),
+        out_shape=jax.ShapeDtypeStruct(shape, partial.dtype),
+        in_specs=[pl.BlockSpec(memory_space=pltpu.VMEM)] * 2,
+        out_specs=pl.BlockSpec(memory_space=pltpu.VMEM),
+        scratch_shapes=[
+            pltpu.VMEM((rows, width), partial.dtype),
+            pltpu.VMEM((rows, width), partial.dtype),
+            dma((count,)), dma((count,)), dma((count,)), dma((ranks,)), dma((2,)), dma((ranks,)), dma((ranks,)),
+        ],
+        compiler_params=pltpu.CompilerParams(
+            collective_id=1, has_side_effects=True, vmem_limit_bytes=40 * 2**20
+        ),
+        name="gather_stream",
+    )(partial, residual)
+    if joined:
+        return stream
+    return stream.transpose(0, 2, 1, 3).reshape(halves * rows, ranks * width)
+
+
+def sums_kernel(
+    ranks, partial, out, twin_part, acc, from_across, from_down, from_up, work, give, got,
+    twin_sent, twin_landed, across_sent, across_landed, up_sent, up_landed, down_sent, down_landed,
+    sum_sent, sum_landed, last_sem,
+):
+    line = Line(ranks)
+    count = line.count
+    line.greet(True)
+    wide = jnp.float32
+
+    def to_twin(block):
+        return send(
+            partial.at[line.twin, block], twin_part.at[block],
+            twin_sent.at[block], twin_landed.at[block], head=line.twin,
+        )
+
+    def to_across(s):
+        return send(
+            acc.at[2 * s + 1 - line.y], from_across.at[s],
+            across_sent.at[s], across_landed.at[s], blk=line.across,
+        )
+
+    def to_up(s):
+        return send(
+            acc.at[2 * s + line.y], from_down.at[s], up_sent.at[s], up_landed.at[s], blk=line.up
+        )
+
+    def to_down(s):
+        return send(
+            acc.at[2 * s + line.y], from_up.at[s], down_sent.at[s], down_landed.at[s], blk=line.down
+        )
+
+    def pair_sum(block):
+        to_twin(block).wait_recv()
+        acc[block] = (partial[line.head, block].astype(wide) + twin_part[block].astype(wide)).astype(
+            acc.dtype
+        )
+
+    def add(block, ref):
+        acc[block] = (acc[block].astype(wide) + ref.astype(wide)).astype(acc.dtype)
+
+    order = []
+    for s in range(count):
+        far = count - 1 - s // 2 if s % 2 == 0 else s // 2
+        order.append(far)
+    for s in order:
+        to_twin(2 * s + 1 - line.y).start()
+    to_twin(ranks).start()
+    for s in order:
+        to_twin(2 * s + line.y).start()
+    for s in order:
+        pair_sum(2 * s + 1 - line.y)
+        to_across(s).start()
+    pair_sum(ranks)
+    sums = LineSum(line, lambda: acc[ranks], work, sum_sent, sum_landed)
+    sums.step(0)
+    for s in order:
+        pair_sum(2 * s + line.y)
+        to_across(s).wait_recv()
+        add(2 * s + line.y, from_across[s])
+
+        @pl.when(s > line.z)
+        def _():
+            @pl.when(line.has_down)
+            def _():
+                to_up(s).wait_recv()
+                add(2 * s + line.y, from_down[s])
+
+            to_up(s).start()
+
+        @pl.when(s < line.z)
+        def _():
+            @pl.when(line.has_up)
+            def _():
+                to_down(s).wait_recv()
+                add(2 * s + line.y, from_up[s])
+
+            to_down(s).start()
+
+    for step in range(1, count):
+        sums.step(step)
+    sums.column()
+    sums.across().start()
+
+    @pl.when(line.has_down)
+    def _():
+        to_up(line.z).wait_recv()
+        add(line.rank, from_down[line.z])
+
+    @pl.when(line.has_up)
+    def _():
+        to_down(line.z).wait_recv()
+        add(line.rank, from_up[line.z])
+
+    spare = sums.total()
+    mine = acc[line.rank].astype(wide)
+    first = line.head == 0
+    give[...] = jnp.where(first, spare, mine).astype(give.dtype)
+    last = send(give, got, last_sem.at[0], last_sem.at[1], head=line.twin)
+    last.start()
+    out[line.head] = jnp.where(first, mine, spare).astype(out.dtype)
+    last.wait_recv()
+    out[line.twin] = got[...]
+    last.wait_send()
+    sums.drain()
+    for block in range(ranks + 1):
+        to_twin(block).wait_send()
+    for s in range(count):
+        to_across(s).wait_send()
+        pl.when(s > line.z)(lambda: to_up(s).wait_send())
+        pl.when(s < line.z)(lambda: to_down(s).wait_send())
+
+
+def scatter_sums(partial, ranks):
+    halves, blocks, rows, width = partial.shape
+    count = ranks // 2
+    dma = pltpu.SemaphoreType.DMA
+
+    def held(*lead):
+        return pltpu.VMEM((*lead, rows, width), partial.dtype)
+
+    return pl.pallas_call(
+        functools.partial(sums_kernel, ranks),
+        out_shape=jax.ShapeDtypeStruct((halves, rows, width), partial.dtype),
+        in_specs=[pl.BlockSpec(memory_space=pltpu.VMEM)],
+        out_specs=pl.BlockSpec(memory_space=pltpu.VMEM),
+        scratch_shapes=[
+            held(blocks), held(blocks), held(count), held(count), held(count), held(6), held(), held(),
+            dma((blocks,)), dma((blocks,)),
+            dma((count,)), dma((count,)), dma((count,)), dma((count,)), dma((count,)), dma((count,)),
+            dma((3,)), dma((3,)), dma((2,)),
+        ],
+        compiler_params=pltpu.CompilerParams(
+            collective_id=2, has_side_effects=True, vmem_limit_bytes=48 * 2**20
+        ),
+        name="scatter_sums",
+    )(partial)
 
 
 def on_device(
@@ -131,6 +526,7 @@
         rows_dev, heads_here * value_weight.shape[2]
     )
     first = rows_dev // 2
+    half = first // 2
     is_full = pick_rank(lives, rank_index) > first
     width = out_weight.shape[1]
     ranks = lax.axis_size("blk")
@@ -142,24 +538,20 @@
         tiled=True,
     )
     full_ranks = (lives > first)[:, None, None]
+    spare_residual = jnp.sum(jnp.where(full_ranks, moved[:, first:], 0).astype(jnp.float32), axis=0)
     residual_rows = jnp.concatenate(
-        [
-            moved[:, :first].reshape(ranks * first, width).astype(jnp.float32),
-            jnp.sum(jnp.where(full_ranks, moved[:, first:], 0).astype(jnp.float32), axis=0),
-        ]
-    )
+        [moved[:, :first], spare_residual.astype(residual.dtype)[None]]
+    )
+    residual_rows = residual_rows.reshape(ranks + 1, 2, half, width).transpose(1, 0, 2, 3)
+    residual_rows = residual_rows.reshape(2, (ranks + 1) * half, width)
     rest = jnp.where(is_full, head_values[first:], 0).astype(jnp.bfloat16)
-    packed = jnp.concatenate(
-        [
-            lax.all_gather(head_values[:first], "blk", axis=0, tiled=True),
-            lax.psum(rest, "blk"),
-        ]
-    )
+    packed = gather_rows(
+        head_values[:first].reshape(2, half, -1), rest.reshape(2, half, -1), ranks
+    )
+    packed = packed.reshape(2 * (ranks + 1) * half, -1)
     partial_out = jnp.dot(packed, out_weight, preferred_element_type=jnp.float32)
-    attended = lax.psum(partial_out.astype(jnp.bfloat16), "head").astype(jnp.float32)
-    stream = lax.all_gather(
-        (residual_rows + attended).astype(jnp.bfloat16), "blk", axis=1, tiled=True
-    )
+    partial_out = partial_out.astype(jnp.bfloat16).reshape(2, (ranks + 1) * half, width)
+    stream = gather_stream(partial_out, residual_rows, ranks)
     wide = stream.astype(jnp.float32)
     scale_rows = lax.rsqrt(jnp.mean(wide * wide, axis=1, keepdims=True) + norm_eps)
     normed = (wide * scale_rows * norm_gain[None, :]).astype(jnp.bfloat16)
@@ -167,17 +559,12 @@
     up_values = jnp.dot(normed, up_weight, preferred_element_type=jnp.float32)
     hidden = (jax.nn.silu(gate_values) * up_values).astype(jnp.bfloat16)
     partial = jnp.dot(hidden, down_weight, preferred_element_type=jnp.float32).astype(jnp.bfloat16)
+    projected = scatter_sums(partial.reshape(2, ranks + 1, half, -1), ranks)
+    projected = projected.reshape(first, -1).astype(jnp.float32)
     head_index = lax.axis_index("head")
-    owned = lax.all_gather(
-        lax.psum_scatter(partial[: ranks * first], ("blk", "head"), scatter_dimension=0, tiled=True),
-        "head",
-        axis=0,
-        tiled=True,
-    )
-    spare = lax.psum(partial[ranks * first :], ("blk", "head"))
-    projected = jnp.where(head_index == 0, owned, spare).astype(jnp.float32)
-    place = jnp.where(head_index == 0, rank_index, ranks) * first
-    stream_half = lax.dynamic_slice_in_dim(stream, place, first, 0).astype(jnp.float32)
+    block = jnp.where(head_index == 0, rank_index, ranks)
+    stream_half = lax.dynamic_slice_in_dim(stream.reshape(2, ranks + 1, half, -1), block, 1, 1)
+    stream_half = stream_half.reshape(first, -1).astype(jnp.float32)
     own_rows = head_index * first + jnp.arange(first, dtype=jnp.int32)
     alive = own_rows < pick_rank(lives, rank_index)
     return jnp.where(alive[:, None], stream_half + projected, 0.0).astype(jnp.bfloat16)

time: 471 us -> 209 us (0.44)
  waiting for transfers between devices: 366 us -> 0.01 us
  Pallas kernels: 0 us -> 130 us
  between operations: 15.1 us -> 1.65 us
  other arithmetic: 16 us -> 11.1 us
    psum x3 -> x0, waiting for transfers between devices: 177 us -> none  [the longest x1 90.4 us: on_device(): spare = lax.psum(partial[ranks * first:], ('blk', 'head'))]
    pallas_call x0 -> x3, Pallas kernels: none -> 130 us  [the longest x1 55.1 us: scatter_sums(): pl.pallas_call(functools.partial(sums_kernel, ranks), out_shape=jax.Shape...]
    all_gather x2 -> x0, waiting for transfers between devices: 124 us -> none  [the longest x1 73.2 us: on_device(): lax.all_gather((residual_rows + attended).astype(jnp.bfloat16), 'blk', ax...]
    reduce_scatter x1 -> x0, waiting for transfers between devices: 64.6 us -> none  [on_device(): lax.psum_scatter(partial[:ranks * first], ('blk', 'head'), scatter_dimens...]
    slice x4 -> x1, local copies, waits for them, and re-layouts: 6.79 us -> 0.11 us  [on_device(): head_values[:first].reshape(2, half, -1)]
  transfers between devices with their start and end apart: 7 -> 1, of which waited for: 6 -> 0; matrix products, arithmetic and copies ran while one was open for 3% -> 17% of each run, Pallas kernels for 0% -> 20%
where the time goes in v2:
time: 209 us
  Pallas kernels  130 us (62%)
  matrix products  46 us (22%)
  local copies, waits for them, and re-layouts  12.8 us (6%)
  other arithmetic  11.1 us (5%)
  starting transfers between devices  7.31 us (3%)
    pallas_call x1, Pallas kernels, scatter_sums(): pl.pallas_call(functools.partial(sums_kernel, ranks), out_shape=jax.Shape...  55.1 us
    pallas_call x1, Pallas kernels, gather_rows(): pl.pallas_call(functools.partial(rows_kernel, ranks), out_shape=jax.Shape...  42.1 us
    pallas_call x1, Pallas kernels, gather_stream(): pl.pallas_call(functools.partial(stream_kernel, ranks), out_shape=jax.Sha...  32.8 us
    dot_general x1, matrix products, on_device(): jnp.dot(hidden, down_weight, preferred_element_type=jnp.float32)  17.6 us
    all_to_all x1, starting transfers between devices, on_device(): lax.all_to_all(residual.reshape(rows_dev, ranks, width).transpose(1, 0, 2...  7.31 us
    dot_general x1, matrix products, on_device(): jnp.einsum('rhl,hlv->rhv', latent_out, value_weight, preferred_element_ty...  6.79 us
    dot_general x1, matrix products, on_device(): jnp.dot(normed, gate_weight, preferred_element_type=jnp.float32)  5.93 us
    dot_general x1, matrix products, on_device(): jnp.dot(packed, out_weight, preferred_element_type=jnp.float32)  5.68 us
  transfers between devices with their start and end apart: 1, of which 0 were waited for; matrix products, arithmetic and copies ran while one was open for 17% of the time, Pallas kernels for 20%

profile of v2, /device:TPU:0, one launch (start us, length us, event | category | flops | bytes accessed | tf_op | source)
XLA Modules:
  0.0 208.9 jit_solution(5053052143910607762)
XLA Ops:
  0.0 1.3 copy.36
  1.4 1.1 copy.32
  2.4 7.3 %all-to-all-start = ((bf16[8,64,896]{2,1,0:T(8,128)(2,1)}), bf16[8,64,896]{2,1,0:T(8,128)(2,1)}, u32[]{:S(2)}, u32[]{:S(2)}) async-start(bf16[8,64,896]{2,1,0:T(8,128)(2,1)} %copy.32), calls=%async_computation | async-start | bytes 1835008 | tf_op jit(solution)/shard_map/all_to_all | solution.py:533
  12.9 4.5 %reshape.146 = bf16[64,32,576]{2,1,0:T(8,128)(2,1)S(1)} reshape(bf16[64,18432]{1,0:T(8,128)(2,1)} %param.14) | data formatting | bytes 4718592 | tf_op jit(solution)/shard_map/reshape | solution.py:511
  18.6 0.9 fusion.69
  19.5 2.0 fusion.5
  22.2 1.0 fusion.9
  23.2 0.8 divide_convert_fusion
  24.7 1.3 compare_and_fusion
  27.3 2.9 %fusion.26 = f32[64,32,512]{2,0,1:T(8,128)} fusion(bf16[64,32,256]{2,1,0:T(8,128)(2,1)S(1)} %divide_convert_fusion, bf16[8,576,256]{2,1,0:T(8,128)(2,1)S(1)} %copy-done.3), kind=kOutput, calls=%fused_computation.30 | convolution fusion | flops 536870912 | bytes 5505024 | tf_op jit(solution)/shard_map/rht,lt->rhl/dot_general | solution.py:48
  30.1 2.7 %fusion.33 = f32[64,32,512]{2,0,1:T(8,128)} fusion(bf16[64,32,64]{2,1,0:T(8,128)(2,1)S(1)} %divide_convert_fusion.1, bf16[576,64]{0,1:T(8,128)(2,1)S(1)} %copy-done.2), kind=kOutput, calls=%fused_computation.39 | convolution fusion | flops 134217728 | bytes 4784128 | tf_op jit(solution)/shard_map/rhj,lj->rhl/dot_general | solution.py:54
  33.4 6.8 %fusion.13 = bf16[64,32,128]{2,0,1:T(8,128)(2,1)S(1)} fusion(bf16[32,512,128]{2,1,0:T(8,128)(2,1)} %param.21, f32[64,32,512]{2,0,1:T(8,128)} %fusion.26, f32[64,32,512]{2,0,1:T(8,128)} %fusion.33, pred[64]{0:T(512)(128)(4,1)S(1)} %iota_compare_fusion.5, bf16[7,32,512]{2,1,0:T(8,128)(2,1)S(1)} %fusion.14, s32[7]{0:T(128)S(1)} %iota_add_fusion, ...), kind=kOutput, calls=%fused_computation.25 | convolution fusion | flops 287572864 | bytes 13336675 | tf_op jit(solution)/shard_map/rhl,hlv->rhv/dot_general | solution.py:522
  41.4 42.1 %gather_rows.1 = bf16[2,9,16,4096]{3,2,1,0:T(8,128)(2,1)S(1)} custom-call(bf16[2,16,4096]{2,1,0:T(8,128)(2,1)S(1)} %reshape.147.own, bf16[2,16,4096]{2,1,0:T(8,128)(2,1)S(1)} %select_n.105.rest), custom_call_target="tpu_custom_call" | custom-call | tf_op jit(solution)/shard_map/gather_rows/pallas_call | solution.py:262
  84.2 5.7 %convolution_convert_fusion.1 = bf16[288,896]{1,0:T(8,128)(2,1)S(1)} fusion(bf16[288,4096]{1,0:T(8,128)(2,1)S(1)} %bitcast.86, bf16[4096,896]{1,0:T(8,128)(2,1)} %param.22), kind=kOutput, calls=%fused_computation.22 | convolution fusion | flops 2114187264 | bytes 10215424 | tf_op jit(solution)/shard_map/dot_general | solution.py:552
  89.9 1.3 fusion.68
  91.3 32.8 %gather_stream.1 = bf16[288,7168]{1,0:T(8,128)(2,1)S(1)} custom-call(bf16[2,144,896]{2,1,0:T(8,128)(2,1)S(1)} %bitcast.88, bf16[2,144,896]{2,1,0:T(8,128)(2,1)S(1)} %bitcast.87), custom_call_target="tpu_custom_call" | custom-call | tf_op jit(solution)/shard_map/gather_stream/pallas_call | solution.py:332
  124.2 0.9 fusion
  125.1 1.0 copy-done
  126.1 5.9 %fusion.18 = f32[288,576]{1,0:T(8,128)S(1)} fusion(bf16[7168,576]{0,1:T(8,128)(2,1)} %param.25, bf16[288,7168]{1,0:T(8,128)(2,1)S(1)} %gather_stream.1, f32[7168]{0:T(1024)S(1)} %copy-done.7, f32[288]{0:T(512)S(1)} %add_rsqrt_fusion), kind=kOutput, calls=%fused_computation.27 | convolution fusion | flops 2386427904 | bytes 13079680 | tf_op jit(solution)/shard_map/dot_general | solution.py:558
  132.0 17.6 %convolution_convert_fusion = bf16[288,7168]{1,0:T(8,128)(2,1)} fusion(bf16[576,7168]{1,0:T(8,128)(2,1)} %param.27, bf16[7168,576]{0,1:T(8,128)(2,1)} %param.26, bf16[288,7168]{1,0:T(8,128)(2,1)} %copy-done, f32[7168]{0:T(1024)S(1)} %copy-done.7, f32[288]{0:T(512)S(1)} %add_rsqrt_fusion, f32[288,576]{1,0:T(8,128)S(1)} %fusion.18), kind=kOutput, calls=%fused_computation.4 | convolution fusion | flops 4767657984 | bytes 25465984 | tf_op jit(solution)/shard_map/dot_general | solution.py:561
  149.7 2.2 %copy-done.1 = bf16[288,7168]{1,0:T(8,128)(2,1)S(1)} copy-done((bf16[288,7168]{1,0:T(8,128)(2,1)S(1)}, bf16[288,7168]{1,0:T(8,128)(2,1)}, u32[]{:S(2)}) %copy-start.1) | copy-done | bytes 4128792
  151.8 55.1 %scatter_sums.1 = bf16[2,16,7168]{2,1,0:T(8,128)(2,1)S(1)} custom-call(bf16[2,9,16,7168]{3,2,1,0:T(8,128)(2,1)S(1)} %bitcast.85), custom_call_target="tpu_custom_call" | custom-call | tf_op jit(solution)/shard_map/scatter_sums/pallas_call | solution.py:473
  206.9 1.1 constant_dynamic-slice_fusion
  208.0 1.0 fusion.29
  (48 shorter events, 8.1 us)
Async XLA Ops:
  0.0 9.8 %copy-start.6 = (s32[8]{0:T(128)S(1)}, s32[8]{0:T(128)}, u32[]{:S(2)}) copy-start(s32[8]{0:T(128)} %param.18) | copy-start | bytes 100
  0.0 9.8 %copy-start.5 = (s32[8]{0:T(128)S(1)}, s32[8]{0:T(128)}, u32[]{:S(2)}) copy-start(s32[8]{0:T(128)} %param.17) | copy-start | bytes 100
  1.4 16.0 %copy-start.2 = (bf16[576,64]{0,1:T(8,128)(2,1)S(1)}, bf16[576,64]{0,1:T(8,128)(2,1)}, u32[]{:S(2)}) copy-start(bf16[576,64]{0,1:T(8,128)(2,1)} %param.16) | copy-start | bytes 221188
  2.4 87.4 %all-to-all-start = ((bf16[8,64,896]{2,1,0:T(8,128)(2,1)}), bf16[8,64,896]{2,1,0:T(8,128)(2,1)}, u32[]{:S(2)}, u32[]{:S(2)}) async-start(bf16[8,64,896]{2,1,0:T(8,128)(2,1)} %copy.32), calls=%async_computation | async-start | bytes 1835008 | tf_op jit(solution)/shard_map/all_to_all | solution.py:533
  21.6 4.5 %copy-start.4 = (s32[1,7]{1,0:T(1,128)S(1)}, s32[1,7]{1,0:T(1,128)}, u32[]{:S(2)}) copy-start(s32[1,7]{1,0:T(1,128)} %param.20) | copy-start | bytes 88
  22.2 4.2 %copy-start.3 = (bf16[8,576,256]{2,1,0:T(8,128)(2,1)S(1)}, bf16[8,576,256]{2,1,0:T(8,128)(2,1)}, u32[]{:S(2)}) copy-start(bf16[8,576,256]{2,1,0:T(8,128)(2,1)} %param.15) | copy-start | bytes 7077892
  91.3 34.8 %copy-start.7 = (f32[7168]{0:T(1024)S(1)}, f32[7168]{0:T(1024)}, u32[]{:S(2)}) copy-start(f32[7168]{0:T(1024)} %param.24) | copy-start | bytes 86020
  124.2 1.9 copy-start
  149.7 2.2 %copy-start.1 = (bf16[288,7168]{1,0:T(8,128)(2,1)S(1)}, bf16[288,7168]{1,0:T(8,128)(2,1)}, u32[]{:S(2)}) copy-start(bf16[288,7168]{1,0:T(8,128)(2,1)} %convolution_convert_fusion) | copy-start | bytes 12386308

commit v3 on v2

--- a/solution.py
+++ b/solution.py
@@ -156,6 +156,7 @@
     to_across(line.z, own).start()
     for step in range(1, line.count):
         low, high = line.z - step, line.z + step
+        between(step)
 
         @pl.when(low >= 0)
         def _():
@@ -173,7 +174,6 @@
             to_across(high, held).start()
             arrived(2 * high + line.y)
 
-        between(step)
     for s in range(line.count):
         slot = 2 * s + 1 - line.y
         send(place(slot), place(slot), across_sem.at[s], landed.at[slot], blk=line.across).wait_recv()
@@ -394,19 +394,24 @@
     for s in range(count):
         far = count - 1 - s // 2 if s % 2 == 0 else s // 2
         order.append(far)
+    to_twin(ranks).start()
     for s in order:
         to_twin(2 * s + 1 - line.y).start()
-    to_twin(ranks).start()
     for s in order:
         to_twin(2 * s + line.y).start()
-    for s in order:
-        pair_sum(2 * s + 1 - line.y)
-        to_across(s).start()
     pair_sum(ranks)
     sums = LineSum(line, lambda: acc[ranks], work, sum_sent, sum_landed)
     sums.step(0)
     for s in order:
+        pair_sum(2 * s + 1 - line.y)
+        to_across(s).start()
+    for index, s in enumerate(order):
         pair_sum(2 * s + line.y)
+        if index > 0:
+            sums.step(index)
+        if index == count - 1:
+            sums.column()
+            sums.across().start()
         to_across(s).wait_recv()
         add(2 * s + line.y, from_across[s])
 
@@ -427,11 +432,6 @@
                 add(2 * s + line.y, from_up[s])
 
             to_down(s).start()
-
-    for step in range(1, count):
-        sums.step(step)
-    sums.column()
-    sums.across().start()
 
     @pl.when(line.has_down)
     def _():
@@ -486,6 +486,72 @@
         ),
         name="scatter_sums",
     )(partial)
+
+
+def mlp_kernel(steps, features, x, gain, gate, up, down, out, gate_sum, up_sum, squares, hidden):
+    step = pl.program_id(0)
+
+    @pl.when(step == 0)
+    def _():
+        gate_sum[...] = jnp.zeros_like(gate_sum)
+        up_sum[...] = jnp.zeros_like(up_sum)
+        squares[...] = jnp.zeros_like(squares)
+
+    @pl.when(step < steps)
+    def _():
+        wide = x[...].astype(jnp.float32)
+        squares[...] += jnp.sum(wide * wide, axis=1, keepdims=True)
+        scaled = (wide * gain[...]).astype(x.dtype)
+        gate_sum[...] += jnp.dot(scaled, gate[...], preferred_element_type=jnp.float32)
+        up_sum[...] += jnp.dot(scaled, up[...], preferred_element_type=jnp.float32)
+
+    @pl.when(step == steps - 1)
+    def _():
+        scale = lax.rsqrt(squares[...] / features + norm_eps)
+        gate_values = gate_sum[...] * scale
+        silu = gate_values / (1.0 + jnp.exp(-gate_values))
+        hidden[...] = (silu * (up_sum[...] * scale)).astype(hidden.dtype)
+
+    @pl.when(step >= steps)
+    def _():
+        out[...] = jnp.dot(hidden[...], down[...], preferred_element_type=jnp.float32).astype(out.dtype)
+
+
+def mlp_partial(stream, gain, gate, up, down):
+    rows, features = stream.shape
+    units = gate.shape[1]
+    tile = next(size for size in (1024, 512, 256, 128, features) if features % size == 0)
+    steps = features // tile
+
+    def early(step):
+        return jnp.minimum(step, steps - 1)
+
+    def late(step):
+        return jnp.maximum(step - steps, 0)
+
+    return pl.pallas_call(
+        functools.partial(mlp_kernel, steps, features),
+        grid=(2 * steps,),
+        out_shape=jax.ShapeDtypeStruct((rows, features), stream.dtype),
+        in_specs=[
+            pl.BlockSpec((rows, tile), lambda i: (0, early(i))),
+            pl.BlockSpec((1, tile), lambda i: (0, early(i))),
+            pl.BlockSpec((tile, units), lambda i: (early(i), 0)),
+            pl.BlockSpec((tile, units), lambda i: (early(i), 0)),
+            pl.BlockSpec((units, tile), lambda i: (0, late(i))),
+        ],
+        out_specs=pl.BlockSpec((rows, tile), lambda i: (0, late(i))),
+        scratch_shapes=[
+            pltpu.VMEM((rows, units), jnp.float32),
+            pltpu.VMEM((rows, units), jnp.float32),
+            pltpu.VMEM((rows, 1), jnp.float32),
+            pltpu.VMEM((rows, units), stream.dtype),
+        ],
+        compiler_params=pltpu.CompilerParams(
+            dimension_semantics=("arbitrary",), vmem_limit_bytes=40 * 2**20
+        ),
+        name="mlp_partial",
+    )(stream, gain[None, :], gate, up, down)
 
 
 def on_device(
@@ -552,13 +618,7 @@
     partial_out = jnp.dot(packed, out_weight, preferred_element_type=jnp.float32)
     partial_out = partial_out.astype(jnp.bfloat16).reshape(2, (ranks + 1) * half, width)
     stream = gather_stream(partial_out, residual_rows, ranks)
-    wide = stream.astype(jnp.float32)
-    scale_rows = lax.rsqrt(jnp.mean(wide * wide, axis=1, keepdims=True) + norm_eps)
-    normed = (wide * scale_rows * norm_gain[None, :]).astype(jnp.bfloat16)
-    gate_values = jnp.dot(normed, gate_weight, preferred_element_type=jnp.float32)
-    up_values = jnp.dot(normed, up_weight, preferred_element_type=jnp.float32)
-    hidden = (jax.nn.silu(gate_values) * up_values).astype(jnp.bfloat16)
-    partial = jnp.dot(hidden, down_weight, preferred_element_type=jnp.float32).astype(jnp.bfloat16)
+    partial = mlp_partial(stream, norm_gain, gate_weight, up_weight, down_weight)
     projected = scatter_sums(partial.reshape(2, ranks + 1, half, -1), ranks)
     projected = projected.reshape(first, -1).astype(jnp.float32)
     head_index = lax.axis_index("head")

time: 209 us -> 214 us (1.024)
  matrix products: 46 us -> 21.5 us
  local copies, waits for them, and re-layouts: 12.8 us -> 33.5 us
  Pallas kernels: 130 us -> 139 us
    dot_general x2 -> x0, matrix products: 23.6 us -> none  [the longest x1 17.6 us: on_device(): jnp.dot(hidden, down_weight, preferred_element_type=jnp.float32)]
    unnamed x17 -> x15, local copies, waits for them, and re-layouts: 4.56 us -> 26.2 us
    pallas_call x0 -> x1, Pallas kernels: none -> 19.3 us  [mlp_partial(): pl.pallas_call(functools.partial(mlp_kernel, steps, features), grid=(2 *...]
    pallas_call x1, Pallas kernels: 55.1 us -> 47.7 us  [scatter_sums(): pl.pallas_call(functools.partial(sums_kernel, ranks), out_shape=jax.Shape...]
    pallas_call x1, Pallas kernels: 42.1 us -> 39.8 us  [gather_rows(): pl.pallas_call(functools.partial(rows_kernel, ranks), out_shape=jax.Shape...]
  transfers between devices with their start and end apart: 1 -> 1, of which waited for: 0 -> 0; matrix products, arithmetic and copies ran while one was open for 17% -> 28% of each run, Pallas kernels for 20% -> 19%
where the time goes in v3:
time: 214 us; the launch traced here: 213 us
  Pallas kernels  139 us (65%)
  local copies, waits for them, and re-layouts  33.5 us (16%)
  matrix products  21.5 us (10%)
  other arithmetic  10.2 us (5%)
  starting transfers between devices  7.31 us (3%)
    pallas_call x1, Pallas kernels, scatter_sums(): pl.pallas_call(functools.partial(sums_kernel, ranks), out_shape=jax.Shape...  47.7 us
    pallas_call x1, Pallas kernels, gather_rows(): pl.pallas_call(functools.partial(rows_kernel, ranks), out_shape=jax.Shape...  39.8 us
    pallas_call x1, Pallas kernels, gather_stream(): pl.pallas_call(functools.partial(stream_kernel, ranks), out_shape=jax.Sha...  31.9 us
    unnamed x15, local copies, waits for them, and re-layouts  26.2 us
    pallas_call x1, Pallas kernels, mlp_partial(): pl.pallas_call(functools.partial(mlp_kernel, steps, features), grid=(2 *...  19.3 us
    all_to_all x1, starting transfers between devices, on_device(): lax.all_to_all(residual.reshape(rows_dev, ranks, width).transpose(1, 0, 2...  7.31 us
    dot_general x1, matrix products, on_device(): jnp.einsum('rhl,hlv->rhv', latent_out, value_weight, preferred_element_ty...  6.79 us
    dot_general x1, matrix products, on_device(): jnp.dot(packed, out_weight, preferred_element_type=jnp.float32)  5.68 us
  transfers between devices with their start and end apart: 1, of which 0 were waited for; matrix products, arithmetic and copies ran while one was open for 28% of the time, Pallas kernels for 19%

profile of v3, /device:TPU:0, one launch (start us, length us, event | category | flops | bytes accessed | tf_op | source)
XLA Modules:
  0.0 213.1 jit_solution(1588978947068837978)
XLA Ops:
  0.0 1.3 copy.44
  1.4 1.1 copy.38
  2.4 7.3 %all-to-all-start = ((bf16[8,64,896]{2,1,0:T(8,128)(2,1)}), bf16[8,64,896]{2,1,0:T(8,128)(2,1)}, u32[]{:S(2)}, u32[]{:S(2)}) async-start(bf16[8,64,896]{2,1,0:T(8,128)(2,1)} %copy.38), calls=%async_computation | async-start | bytes 1835008 | tf_op jit(solution)/shard_map/all_to_all | solution.py:599
  9.8 0.7 select_reduce_fusion.2
  11.1 4.5 %reshape.137 = bf16[64,32,576]{2,1,0:T(8,128)(2,1)S(1)} reshape(bf16[64,18432]{1,0:T(8,128)(2,1)} %param.14) | data formatting | bytes 4718592 | tf_op jit(solution)/shard_map/reshape | solution.py:577
  17.6 0.9 fusion.62
  18.6 1.1 fusion.2
  20.4 1.0 fusion.6
  21.4 0.7 divide_convert_fusion.1
  22.1 0.8 divide_convert_fusion
  24.0 1.3 compare_and_fusion
  26.5 2.7 %fusion.26 = f32[64,32,512]{2,0,1:T(8,128)} fusion(bf16[64,32,64]{2,1,0:T(8,128)(2,1)S(1)} %divide_convert_fusion.1, bf16[576,64]{0,1:T(8,128)(2,1)S(1)} %copy-done.1), kind=kOutput, calls=%fused_computation.30 | convolution fusion | flops 134217728 | bytes 4784128 | tf_op jit(solution)/shard_map/rhj,lj->rhl/dot_general | solution.py:54
  29.2 2.9 %fusion.19 = f32[64,32,512]{2,0,1:T(8,128)} fusion(bf16[64,32,256]{2,1,0:T(8,128)(2,1)S(1)} %divide_convert_fusion, bf16[8,576,256]{2,1,0:T(8,128)(2,1)S(1)} %copy-done.2), kind=kOutput, calls=%fused_computation.21 | convolution fusion | flops 536870912 | bytes 5505024 | tf_op jit(solution)/shard_map/rht,lt->rhl/dot_general | solution.py:48
  32.7 6.8 %fusion.9 = bf16[64,32,128]{2,0,1:T(8,128)(2,1)S(1)} fusion(bf16[32,512,128]{2,1,0:T(8,128)(2,1)} %param.21, f32[64,32,512]{2,0,1:T(8,128)} %fusion.19, f32[64,32,512]{2,0,1:T(8,128)} %fusion.26, pred[64]{0:T(512)(128)(4,1)S(1)} %iota_compare_fusion.5, bf16[7,32,512]{2,1,0:T(8,128)(2,1)S(1)} %fusion.10, s32[7]{0:T(128)S(1)} %iota_add_fusion, ...), kind=kOutput, calls=%fused_computation.17 | convolution fusion | flops 287572864 | bytes 13336675 | tf_op jit(solution)/shard_map/rhl,hlv->rhv/dot_general | solution.py:588
  40.7 12.4 %copy.40.gate = bf16[7168,576]{1,0:T(8,128)(2,1)} copy(bf16[7168,576]{0,1:T(8,128)(2,1)} %param.25) | data formatting | bytes 16515072 | tf_op args[11]
  53.1 12.4 %copy.41.up = bf16[7168,576]{1,0:T(8,128)(2,1)} copy(bf16[7168,576]{0,1:T(8,128)(2,1)} %param.26) | data formatting | bytes 16515072 | tf_op args[12]
  65.5 39.8 %gather_rows.1 = bf16[2,9,16,4096]{3,2,1,0:T(8,128)(2,1)S(1)} custom-call(bf16[2,16,4096]{2,1,0:T(8,128)(2,1)S(1)} %reshape.138.own, bf16[2,16,4096]{2,1,0:T(8,128)(2,1)S(1)} %select_n.105.rest), custom_call_target="tpu_custom_call" | custom-call | tf_op jit(solution)/shard_map/gather_rows/pallas_call | solution.py:262
  105.2 0.7 add_compare_fusion
  106.0 5.7 %convolution_convert_fusion = bf16[288,896]{1,0:T(8,128)(2,1)S(1)} fusion(bf16[288,4096]{1,0:T(8,128)(2,1)S(1)} %bitcast.79, bf16[4096,896]{1,0:T(8,128)(2,1)} %param.22), kind=kOutput, calls=%fused_computation.16 | convolution fusion | flops 2114187264 | bytes 10215424 | tf_op jit(solution)/shard_map/dot_general | solution.py:618
  111.7 1.3 fusion.61
  113.1 31.9 %gather_stream.1.x = bf16[288,7168]{1,0:T(8,128)(2,1)S(1)} custom-call(bf16[2,144,896]{2,1,0:T(8,128)(2,1)S(1)} %bitcast.81, bf16[2,144,896]{2,1,0:T(8,128)(2,1)S(1)} %bitcast.80), custom_call_target="tpu_custom_call" | custom-call | tf_op jit(solution)/shard_map/gather_stream/pallas_call | solution.py:332
  145.0 19.3 %mlp_partial.1 = bf16[288,7168]{1,0:T(8,128)(2,1)S(1)} custom-call(bf16[288,7168]{1,0:T(8,128)(2,1)S(1)} %gather_stream.1.x, f32[1,7168]{1,0:T(1,128)S(1)} %bitcast.82, bf16[7168,576]{1,0:T(8,128)(2,1)} %copy.40.gate, bf16[7168,576]{1,0:T(8,128)(2,1)} %copy.41.up, bf16[576,7168]{1,0:T(8,128)(2,1)} %down.1), custom_call_target="tpu_custom_call" | custom-call | tf_op jit(solution)/shard_map/mlp_partial/pallas_call | solution.py:532
  164.3 47.7 %scatter_sums.1 = bf16[2,16,7168]{2,1,0:T(8,128)(2,1)S(1)} custom-call(bf16[2,9,16,7168]{3,2,1,0:T(8,128)(2,1)S(1)} %bitcast.78), custom_call_target="tpu_custom_call" | custom-call | tf_op jit(solution)/shard_map/scatter_sums/pallas_call | solution.py:473
  212.1 1.0 fusion.22
  (43 shorter events, 6.1 us)
Async XLA Ops:
  0.0 9.8 %copy-start.4 = (s32[8]{0:T(128)S(1)}, s32[8]{0:T(128)}, u32[]{:S(2)}) copy-start(s32[8]{0:T(128)} %param.17) | copy-start | bytes 100
  0.0 9.8 %copy-start.5 = (s32[8]{0:T(128)S(1)}, s32[8]{0:T(128)}, u32[]{:S(2)}) copy-start(s32[8]{0:T(128)} %param.18) | copy-start | bytes 100
  2.4 109.2 %all-to-all-start = ((bf16[8,64,896]{2,1,0:T(8,128)(2,1)}), bf16[8,64,896]{2,1,0:T(8,128)(2,1)}, u32[]{:S(2)}, u32[]{:S(2)}) async-start(bf16[8,64,896]{2,1,0:T(8,128)(2,1)} %copy.38), calls=%async_computation | async-start | bytes 1835008 | tf_op jit(solution)/shard_map/all_to_all | solution.py:599
  11.1 4.5 %copy-start.1 = (bf16[576,64]{0,1:T(8,128)(2,1)S(1)}, bf16[576,64]{0,1:T(8,128)(2,1)}, u32[]{:S(2)}) copy-start(bf16[576,64]{0,1:T(8,128)(2,1)} %param.16) | copy-start | bytes 221188
  16.8 1.8 copy-start.2
  21.3 3.9 %copy-start.3 = (s32[1,7]{1,0:T(1,128)S(1)}, s32[1,7]{1,0:T(1,128)}, u32[]{:S(2)}) copy-start(s32[1,7]{1,0:T(1,128)} %param.20) | copy-start | bytes 88
  113.1 32.0 %copy-start = (f32[7168]{0:T(1024)S(1)}, f32[7168]{0:T(1024)}, u32[]{:S(2)}) copy-start(f32[7168]{0:T(1024)} %param.24) | copy-start | bytes 86020

commit v4 on v3

--- a/solution.py
+++ b/solution.py
@@ -502,8 +502,11 @@
         wide = x[...].astype(jnp.float32)
         squares[...] += jnp.sum(wide * wide, axis=1, keepdims=True)
         scaled = (wide * gain[...]).astype(x.dtype)
-        gate_sum[...] += jnp.dot(scaled, gate[...], preferred_element_type=jnp.float32)
-        up_sum[...] += jnp.dot(scaled, up[...], preferred_element_type=jnp.float32)
+        last = (((1,), (1,)), ((), ()))
+        gate_sum[...] += lax.dot_general(
+            scaled, gate[...], last, preferred_element_type=jnp.float32
+        )
+        up_sum[...] += lax.dot_general(scaled, up[...], last, preferred_element_type=jnp.float32)
 
     @pl.when(step == steps - 1)
     def _():
@@ -536,8 +539,8 @@
         in_specs=[
             pl.BlockSpec((rows, tile), lambda i: (0, early(i))),
             pl.BlockSpec((1, tile), lambda i: (0, early(i))),
-            pl.BlockSpec((tile, units), lambda i: (early(i), 0)),
-            pl.BlockSpec((tile, units), lambda i: (early(i), 0)),
+            pl.BlockSpec((units, tile), lambda i: (0, early(i))),
+            pl.BlockSpec((units, tile), lambda i: (0, early(i))),
             pl.BlockSpec((units, tile), lambda i: (0, late(i))),
         ],
         out_specs=pl.BlockSpec((rows, tile), lambda i: (0, late(i))),
@@ -551,7 +554,7 @@
             dimension_semantics=("arbitrary",), vmem_limit_bytes=40 * 2**20
         ),
         name="mlp_partial",
-    )(stream, gain[None, :], gate, up, down)
+    )(stream, gain[None, :], gate.T, up.T, down)
 
 
 def on_device(

time: 214 us -> 189 us (0.88)
  local copies, waits for them, and re-layouts: 33.5 us -> 9.38 us
    unnamed x15 -> x13, local copies, waits for them, and re-layouts: 26.2 us -> 2.1 us
  transfers between devices with their start and end apart: 1 -> 1, of which waited for: 0 -> 0; matrix products, arithmetic and copies ran while one was open for 28% -> 19% of each run, Pallas kernels for 19% -> 21%
where the time goes in v4:
time: 189 us; the launch traced here: 188 us
  Pallas kernels  138 us (73%)
  matrix products  21.5 us (11%)
  other arithmetic  10.2 us (5%)
  local copies, waits for them, and re-layouts  9.38 us (5%)
  starting transfers between devices  7.31 us (4%)
    pallas_call x1, Pallas kernels, scatter_sums(): pl.pallas_call(functools.partial(sums_kernel, ranks), out_shape=jax.Shape...  47.6 us
    pallas_call x1, Pallas kernels, gather_rows(): pl.pallas_call(functools.partial(rows_kernel, ranks), out_shape=jax.Shape...  39.8 us
    pallas_call x1, Pallas kernels, gather_stream(): pl.pallas_call(functools.partial(stream_kernel, ranks), out_shape=jax.Sha...  31.9 us
    pallas_call x1, Pallas kernels, mlp_partial(): pl.pallas_call(functools.partial(mlp_kernel, steps, features), grid=(2 *...  19.1 us
    all_to_all x1, starting transfers between devices, on_device(): lax.all_to_all(residual.reshape(rows_dev, ranks, width).transpose(1, 0, 2...  7.31 us
    dot_general x1, matrix products, on_device(): jnp.einsum('rhl,hlv->rhv', latent_out, value_weight, preferred_element_ty...  6.79 us
    dot_general x1, matrix products, on_device(): jnp.dot(packed, out_weight, preferred_element_type=jnp.float32)  5.68 us
    reshape x1, local copies, waits for them, and re-layouts, on_device(): queries.reshape(rows_dev, heads_here, queries.shape[1] // heads_here)  4.52 us
  transfers between devices with their start and end apart: 1, of which 0 were waited for; matrix products, arithmetic and copies ran while one was open for 19% of the time, Pallas kernels for 21%

profile of v4, /device:TPU:0, one launch (start us, length us, event | category | flops | bytes accessed | tf_op | source)
XLA Modules:
  0.0 188.5 jit_solution(7274292778261557058)
XLA Ops:
  0.0 1.3 copy.36
  1.4 1.1 copy.32
  2.4 7.3 %all-to-all-start = ((bf16[8,64,896]{2,1,0:T(8,128)(2,1)}), bf16[8,64,896]{2,1,0:T(8,128)(2,1)}, u32[]{:S(2)}, u32[]{:S(2)}) async-start(bf16[8,64,896]{2,1,0:T(8,128)(2,1)} %copy.32), calls=%async_computation | async-start | bytes 1835008 | tf_op jit(solution)/shard_map/all_to_all | solution.py:602
  9.8 0.7 select_reduce_fusion.2
  12.9 4.5 %reshape.137 = bf16[64,32,576]{2,1,0:T(8,128)(2,1)S(1)} reshape(bf16[64,18432]{1,0:T(8,128)(2,1)} %param.14) | data formatting | bytes 4718592 | tf_op jit(solution)/shard_map/reshape | solution.py:580
  18.6 0.9 fusion.62
  19.6 0.7 copy-done.2
  20.3 1.1 fusion.2
  21.4 0.7 fusion.23
  22.0 1.0 fusion.6
  23.0 0.8 divide_convert_fusion
  23.8 0.7 divide_convert_fusion.1
  24.6 1.3 compare_and_fusion
  27.1 2.9 %fusion.19 = f32[64,32,512]{2,0,1:T(8,128)} fusion(bf16[64,32,256]{2,1,0:T(8,128)(2,1)S(1)} %divide_convert_fusion, bf16[8,576,256]{2,1,0:T(8,128)(2,1)S(1)} %copy-done.2), kind=kOutput, calls=%fused_computation.21 | convolution fusion | flops 536870912 | bytes 5505024 | tf_op jit(solution)/shard_map/rht,lt->rhl/dot_general | solution.py:48
  29.9 2.7 %fusion.26 = f32[64,32,512]{2,0,1:T(8,128)} fusion(bf16[64,32,64]{2,1,0:T(8,128)(2,1)S(1)} %divide_convert_fusion.1, bf16[576,64]{0,1:T(8,128)(2,1)S(1)} %copy-done.1), kind=kOutput, calls=%fused_computation.30 | convolution fusion | flops 134217728 | bytes 4784128 | tf_op jit(solution)/shard_map/rhj,lj->rhl/dot_general | solution.py:54
  33.3 6.8 %fusion.9 = bf16[64,32,128]{2,0,1:T(8,128)(2,1)S(1)} fusion(bf16[32,512,128]{2,1,0:T(8,128)(2,1)} %param.21, f32[64,32,512]{2,0,1:T(8,128)} %fusion.19, f32[64,32,512]{2,0,1:T(8,128)} %fusion.26, pred[64]{0:T(512)(128)(4,1)S(1)} %iota_compare_fusion.5, bf16[7,32,512]{2,1,0:T(8,128)(2,1)S(1)} %fusion.10, s32[7]{0:T(128)S(1)} %iota_add_fusion, ...), kind=kOutput, calls=%fused_computation.17 | convolution fusion | flops 287572864 | bytes 13336675 | tf_op jit(solution)/shard_map/rhl,hlv->rhv/dot_general | solution.py:591
  41.2 39.8 %gather_rows.1 = bf16[2,9,16,4096]{3,2,1,0:T(8,128)(2,1)S(1)} custom-call(bf16[2,16,4096]{2,1,0:T(8,128)(2,1)S(1)} %reshape.138.own, bf16[2,16,4096]{2,1,0:T(8,128)(2,1)S(1)} %select_n.105.rest), custom_call_target="tpu_custom_call" | custom-call | tf_op jit(solution)/shard_map/gather_rows/pallas_call | solution.py:262
  81.0 0.6 add_compare_fusion
  81.7 5.7 %convolution_convert_fusion = bf16[288,896]{1,0:T(8,128)(2,1)S(1)} fusion(bf16[288,4096]{1,0:T(8,128)(2,1)S(1)} %bitcast.81, bf16[4096,896]{1,0:T(8,128)(2,1)} %param.22), kind=kOutput, calls=%fused_computation.16 | convolution fusion | flops 2114187264 | bytes 10215424 | tf_op jit(solution)/shard_map/dot_general | solution.py:621
  87.4 1.3 fusion.61
  88.8 31.9 %gather_stream.1.x = bf16[288,7168]{1,0:T(8,128)(2,1)S(1)} custom-call(bf16[2,144,896]{2,1,0:T(8,128)(2,1)S(1)} %bitcast.83, bf16[2,144,896]{2,1,0:T(8,128)(2,1)S(1)} %bitcast.82), custom_call_target="tpu_custom_call" | custom-call | tf_op jit(solution)/shard_map/gather_stream/pallas_call | solution.py:332
  120.7 19.1 %mlp_partial.1 = bf16[288,7168]{1,0:T(8,128)(2,1)S(1)} custom-call(bf16[288,7168]{1,0:T(8,128)(2,1)S(1)} %gather_stream.1.x, f32[1,7168]{1,0:T(1,128)S(1)} %bitcast.84, bf16[576,7168]{1,0:T(8,128)(2,1)} %bitcast.85, bf16[576,7168]{1,0:T(8,128)(2,1)} %bitcast.86, bf16[576,7168]{1,0:T(8,128)(2,1)} %down.1), custom_call_target="tpu_custom_call" | custom-call | tf_op jit(solution)/shard_map/mlp_partial/pallas_call | solution.py:535
  139.9 47.6 %scatter_sums.1 = bf16[2,16,7168]{2,1,0:T(8,128)(2,1)S(1)} custom-call(bf16[2,9,16,7168]{3,2,1,0:T(8,128)(2,1)S(1)} %bitcast.80), custom_call_target="tpu_custom_call" | custom-call | tf_op jit(solution)/shard_map/scatter_sums/pallas_call | solution.py:473
  187.5 1.0 fusion.22
  (41 shorter events, 5.4 us)
Async XLA Ops:
  0.0 9.7 %copy-start.4 = (s32[8]{0:T(128)S(1)}, s32[8]{0:T(128)}, u32[]{:S(2)}) copy-start(s32[8]{0:T(128)} %param.17) | copy-start | bytes 100
  0.0 9.7 %copy-start.5 = (s32[8]{0:T(128)S(1)}, s32[8]{0:T(128)}, u32[]{:S(2)}) copy-start(s32[8]{0:T(128)} %param.18) | copy-start | bytes 100
  2.4 85.0 %all-to-all-start = ((bf16[8,64,896]{2,1,0:T(8,128)(2,1)}), bf16[8,64,896]{2,1,0:T(8,128)(2,1)}, u32[]{:S(2)}, u32[]{:S(2)}) async-start(bf16[8,64,896]{2,1,0:T(8,128)(2,1)} %copy.32), calls=%async_computation | async-start | bytes 1835008 | tf_op jit(solution)/shard_map/all_to_all | solution.py:602
  12.9 4.5 %copy-start.1 = (bf16[576,64]{0,1:T(8,128)(2,1)S(1)}, bf16[576,64]{0,1:T(8,128)(2,1)}, u32[]{:S(2)}) copy-start(bf16[576,64]{0,1:T(8,128)(2,1)} %param.16) | copy-start | bytes 221188
  18.6 1.7 copy-start.2
  23.0 2.8 %copy-start.3 = (s32[1,7]{1,0:T(1,128)S(1)}, s32[1,7]{1,0:T(1,128)}, u32[]{:S(2)}) copy-start(s32[1,7]{1,0:T(1,128)} %param.20) | copy-start | bytes 88
  88.8 31.9 %copy-start = (f32[7168]{0:T(1024)S(1)}, f32[7168]{0:T(1024)}, u32[]{:S(2)}) copy-start(f32[7168]{0:T(1024)} %param.24) | copy-start | bytes 86020

commit v5 on v4

--- a/solution.py
+++ b/solution.py
@@ -365,20 +365,31 @@
             twin_sent.at[block], twin_landed.at[block], head=line.twin,
         )
 
-    def to_across(s):
+    pieces = 2
+    part = out.shape[2] // pieces
+
+    def columns(piece):
+        return pl.ds(piece * part, part)
+
+    def to_across(s, piece):
+        index = s * pieces + piece
         return send(
-            acc.at[2 * s + 1 - line.y], from_across.at[s],
-            across_sent.at[s], across_landed.at[s], blk=line.across,
-        )
-
-    def to_up(s):
+            acc.at[2 * s + 1 - line.y, :, columns(piece)], from_across.at[s, :, columns(piece)],
+            across_sent.at[index], across_landed.at[index], blk=line.across,
+        )
+
+    def to_up(s, piece):
+        index = s * pieces + piece
         return send(
-            acc.at[2 * s + line.y], from_down.at[s], up_sent.at[s], up_landed.at[s], blk=line.up
-        )
-
-    def to_down(s):
+            acc.at[2 * s + line.y, :, columns(piece)], from_down.at[s, :, columns(piece)],
+            up_sent.at[index], up_landed.at[index], blk=line.up,
+        )
+
+    def to_down(s, piece):
+        index = s * pieces + piece
         return send(
-            acc.at[2 * s + line.y], from_up.at[s], down_sent.at[s], down_landed.at[s], blk=line.down
+            acc.at[2 * s + line.y, :, columns(piece)], from_up.at[s, :, columns(piece)],
+            down_sent.at[index], down_landed.at[index], blk=line.down,
         )
 
     def pair_sum(block):
@@ -387,8 +398,9 @@
             acc.dtype
         )
 
-    def add(block, ref):
-        acc[block] = (acc[block].astype(wide) + ref.astype(wide)).astype(acc.dtype)
+    def add(block, held, s, piece):
+        total = acc[block, :, columns(piece)].astype(wide) + held[s, :, columns(piece)].astype(wide)
+        acc[block, :, columns(piece)] = total.astype(acc.dtype)
 
     order = []
     for s in range(count):
@@ -404,7 +416,8 @@
     sums.step(0)
     for s in order:
         pair_sum(2 * s + 1 - line.y)
-        to_across(s).start()
+        for piece in range(pieces):
+            to_across(s, piece).start()
     for index, s in enumerate(order):
         pair_sum(2 * s + line.y)
         if index > 0:
@@ -412,36 +425,39 @@
         if index == count - 1:
             sums.column()
             sums.across().start()
-        to_across(s).wait_recv()
-        add(2 * s + line.y, from_across[s])
-
-        @pl.when(s > line.z)
+        for piece in range(pieces):
+            to_across(s, piece).wait_recv()
+            add(2 * s + line.y, from_across, s, piece)
+
+            @pl.when(s > line.z)
+            def _():
+                @pl.when(line.has_down)
+                def _():
+                    to_up(s, piece).wait_recv()
+                    add(2 * s + line.y, from_down, s, piece)
+
+                to_up(s, piece).start()
+
+            @pl.when(s < line.z)
+            def _():
+                @pl.when(line.has_up)
+                def _():
+                    to_down(s, piece).wait_recv()
+                    add(2 * s + line.y, from_up, s, piece)
+
+                to_down(s, piece).start()
+
+    for piece in range(pieces):
+
+        @pl.when(line.has_down)
         def _():
-            @pl.when(line.has_down)
-            def _():
-                to_up(s).wait_recv()
-                add(2 * s + line.y, from_down[s])
-
-            to_up(s).start()
-
-        @pl.when(s < line.z)
+            to_up(line.z, piece).wait_recv()
+            add(line.rank, from_down, line.z, piece)
+
+        @pl.when(line.has_up)
         def _():
-            @pl.when(line.has_up)
-            def _():
-                to_down(s).wait_recv()
-                add(2 * s + line.y, from_up[s])
-
-            to_down(s).start()
-
-    @pl.when(line.has_down)
-    def _():
-        to_up(line.z).wait_recv()
-        add(line.rank, from_down[line.z])
-
-    @pl.when(line.has_up)
-    def _():
-        to_down(line.z).wait_recv()
-        add(line.rank, from_up[line.z])
+            to_down(line.z, piece).wait_recv()
+            add(line.rank, from_up, line.z, piece)
 
     spare = sums.total()
     mine = acc[line.rank].astype(wide)
@@ -457,9 +473,10 @@
     for block in range(ranks + 1):
         to_twin(block).wait_send()
     for s in range(count):
-        to_across(s).wait_send()
-        pl.when(s > line.z)(lambda: to_up(s).wait_send())
-        pl.when(s < line.z)(lambda: to_down(s).wait_send())
+        for piece in range(pieces):
+            to_across(s, piece).wait_send()
+            pl.when(s > line.z)(lambda: to_up(s, piece).wait_send())
+            pl.when(s < line.z)(lambda: to_down(s, piece).wait_send())
 
 
 def scatter_sums(partial, ranks):
@@ -478,7 +495,7 @@
         scratch_shapes=[
             held(blocks), held(blocks), held(count), held(count), held(count), held(6), held(), held(),
             dma((blocks,)), dma((blocks,)),
-            dma((count,)), dma((count,)), dma((count,)), dma((count,)), dma((count,)), dma((count,)),
+            *[dma((2 * count,))] * 6,
             dma((3,)), dma((3,)), dma((2,)),
         ],
         compiler_params=pltpu.CompilerParams(

time: 189 us -> 186 us (0.984)
  Pallas kernels: 138 us -> 134 us
    pallas_call x1, Pallas kernels: 47.6 us -> 43.5 us  [scatter_sums(): pl.pallas_call(functools.partial(sums_kernel, ranks), out_shape=jax.Shape...]
  transfers between devices with their start and end apart: 1 -> 1, of which waited for: 0 -> 0; matrix products, arithmetic and copies ran while one was open for 19% -> 19% of each run, Pallas kernels for 21% -> 22%
where the time goes in v5:
time: 186 us; the launch traced here: 184 us
  Pallas kernels  134 us (72%)
  matrix products  21.5 us (12%)
  other arithmetic  10.2 us (5%)
  local copies, waits for them, and re-layouts  9.39 us (5%)
  starting transfers between devices  7.31 us (4%)
    pallas_call x1, Pallas kernels, scatter_sums(): pl.pallas_call(functools.partial(sums_kernel, ranks), out_shape=jax.Shape...  43.5 us
    pallas_call x1, Pallas kernels, gather_rows(): pl.pallas_call(functools.partial(rows_kernel, ranks), out_shape=jax.Shape...  39.8 us
    pallas_call x1, Pallas kernels, gather_stream(): pl.pallas_call(functools.partial(stream_kernel, ranks), out_shape=jax.Sha...  31.9 us
    pallas_call x1, Pallas kernels, mlp_partial(): pl.pallas_call(functools.partial(mlp_kernel, steps, features), grid=(2 *...  19.1 us
    all_to_all x1, starting transfers between devices, on_device(): lax.all_to_all(residual.reshape(rows_dev, ranks, width).transpose(1, 0, 2...  7.31 us
    dot_general x1, matrix products, on_device(): jnp.einsum('rhl,hlv->rhv', latent_out, value_weight, preferred_element_ty...  6.79 us
    dot_general x1, matrix products, on_device(): jnp.dot(packed, out_weight, preferred_element_type=jnp.float32)  5.68 us
    reshape x1, local copies, waits for them, and re-layouts, on_device(): queries.reshape(rows_dev, heads_here, queries.shape[1] // heads_here)  4.52 us
  transfers between devices with their start and end apart: 1, of which 0 were waited for; matrix products, arithmetic and copies ran while one was open for 19% of the time, Pallas kernels for 22%

profile of v5, /device:TPU:0, one launch (start us, length us, event | category | flops | bytes accessed | tf_op | source)
XLA Modules:
  0.0 184.4 jit_solution(15510888284114350909)
XLA Ops:
  0.0 1.3 copy.36
  1.4 1.1 copy.32
  2.4 7.3 %all-to-all-start = ((bf16[8,64,896]{2,1,0:T(8,128)(2,1)}), bf16[8,64,896]{2,1,0:T(8,128)(2,1)}, u32[]{:S(2)}, u32[]{:S(2)}) async-start(bf16[8,64,896]{2,1,0:T(8,128)(2,1)} %copy.32), calls=%async_computation | async-start | bytes 1835008 | tf_op jit(solution)/shard_map/all_to_all | solution.py:619
  9.8 0.7 select_reduce_fusion.2
  12.9 4.5 %reshape.137 = bf16[64,32,576]{2,1,0:T(8,128)(2,1)S(1)} reshape(bf16[64,18432]{1,0:T(8,128)(2,1)} %param.14) | data formatting | bytes 4718592 | tf_op jit(solution)/shard_map/reshape | solution.py:597
  18.6 0.9 fusion.62
  19.6 0.7 copy-done.2
  20.3 1.1 fusion.2
  21.4 0.7 fusion.23
  22.0 1.0 fusion.6
  23.0 0.8 divide_convert_fusion
  23.8 0.7 divide_convert_fusion.1
  24.6 1.3 compare_and_fusion
  27.1 2.9 %fusion.19 = f32[64,32,512]{2,0,1:T(8,128)} fusion(bf16[64,32,256]{2,1,0:T(8,128)(2,1)S(1)} %divide_convert_fusion, bf16[8,576,256]{2,1,0:T(8,128)(2,1)S(1)} %copy-done.2), kind=kOutput, calls=%fused_computation.21 | convolution fusion | flops 536870912 | bytes 5505024 | tf_op jit(solution)/shard_map/rht,lt->rhl/dot_general | solution.py:48
  30.0 2.7 %fusion.26 = f32[64,32,512]{2,0,1:T(8,128)} fusion(bf16[64,32,64]{2,1,0:T(8,128)(2,1)S(1)} %divide_convert_fusion.1, bf16[576,64]{0,1:T(8,128)(2,1)S(1)} %copy-done.1), kind=kOutput, calls=%fused_computation.30 | convolution fusion | flops 134217728 | bytes 4784128 | tf_op jit(solution)/shard_map/rhj,lj->rhl/dot_general | solution.py:54
  33.3 6.8 %fusion.9 = bf16[64,32,128]{2,0,1:T(8,128)(2,1)S(1)} fusion(bf16[32,512,128]{2,1,0:T(8,128)(2,1)} %param.21, f32[64,32,512]{2,0,1:T(8,128)} %fusion.19, f32[64,32,512]{2,0,1:T(8,128)} %fusion.26, pred[64]{0:T(512)(128)(4,1)S(1)} %iota_compare_fusion.5, bf16[7,32,512]{2,1,0:T(8,128)(2,1)S(1)} %fusion.10, s32[7]{0:T(128)S(1)} %iota_add_fusion, ...), kind=kOutput, calls=%fused_computation.17 | convolution fusion | flops 287572864 | bytes 13336675 | tf_op jit(solution)/shard_map/rhl,hlv->rhv/dot_general | solution.py:608
  41.2 39.8 %gather_rows.1 = bf16[2,9,16,4096]{3,2,1,0:T(8,128)(2,1)S(1)} custom-call(bf16[2,16,4096]{2,1,0:T(8,128)(2,1)S(1)} %reshape.138.own, bf16[2,16,4096]{2,1,0:T(8,128)(2,1)S(1)} %select_n.105.rest), custom_call_target="tpu_custom_call" | custom-call | tf_op jit(solution)/shard_map/gather_rows/pallas_call | solution.py:262
  81.0 0.6 add_compare_fusion
  81.7 5.7 %convolution_convert_fusion = bf16[288,896]{1,0:T(8,128)(2,1)S(1)} fusion(bf16[288,4096]{1,0:T(8,128)(2,1)S(1)} %bitcast.81, bf16[4096,896]{1,0:T(8,128)(2,1)} %param.22), kind=kOutput, calls=%fused_computation.16 | convolution fusion | flops 2114187264 | bytes 10215424 | tf_op jit(solution)/shard_map/dot_general | solution.py:638
  87.4 1.3 fusion.61
  88.8 31.9 %gather_stream.1.x = bf16[288,7168]{1,0:T(8,128)(2,1)S(1)} custom-call(bf16[2,144,896]{2,1,0:T(8,128)(2,1)S(1)} %bitcast.83, bf16[2,144,896]{2,1,0:T(8,128)(2,1)S(1)} %bitcast.82), custom_call_target="tpu_custom_call" | custom-call | tf_op jit(solution)/shard_map/gather_stream/pallas_call | solution.py:332
  120.7 19.1 %mlp_partial.1 = bf16[288,7168]{1,0:T(8,128)(2,1)S(1)} custom-call(bf16[288,7168]{1,0:T(8,128)(2,1)S(1)} %gather_stream.1.x, f32[1,7168]{1,0:T(1,128)S(1)} %bitcast.84, bf16[576,7168]{1,0:T(8,128)(2,1)} %bitcast.85, bf16[576,7168]{1,0:T(8,128)(2,1)} %bitcast.86, bf16[576,7168]{1,0:T(8,128)(2,1)} %down.1), custom_call_target="tpu_custom_call" | custom-call | tf_op jit(solution)/shard_map/mlp_partial/pallas_call | solution.py:552
  139.9 43.5 %scatter_sums.1 = bf16[2,16,7168]{2,1,0:T(8,128)(2,1)S(1)} custom-call(bf16[2,9,16,7168]{3,2,1,0:T(8,128)(2,1)S(1)} %bitcast.80), custom_call_target="tpu_custom_call" | custom-call | tf_op jit(solution)/shard_map/scatter_sums/pallas_call | solution.py:490
  183.4 1.0 fusion.22
  (41 shorter events, 5.4 us)
Async XLA Ops:
  0.0 9.7 %copy-start.4 = (s32[8]{0:T(128)S(1)}, s32[8]{0:T(128)}, u32[]{:S(2)}) copy-start(s32[8]{0:T(128)} %param.17) | copy-start | bytes 100
  0.0 9.7 %copy-start.5 = (s32[8]{0:T(128)S(1)}, s32[8]{0:T(128)}, u32[]{:S(2)}) copy-start(s32[8]{0:T(128)} %param.18) | copy-start | bytes 100
  2.4 85.0 %all-to-all-start = ((bf16[8,64,896]{2,1,0:T(8,128)(2,1)}), bf16[8,64,896]{2,1,0:T(8,128)(2,1)}, u32[]{:S(2)}, u32[]{:S(2)}) async-start(bf16[8,64,896]{2,1,0:T(8,128)(2,1)} %copy.32), calls=%async_computation | async-start | bytes 1835008 | tf_op jit(solution)/shard_map/all_to_all | solution.py:619
  12.9 4.5 %copy-start.1 = (bf16[576,64]{0,1:T(8,128)(2,1)S(1)}, bf16[576,64]{0,1:T(8,128)(2,1)}, u32[]{:S(2)}) copy-start(bf16[576,64]{0,1:T(8,128)(2,1)} %param.16) | copy-start | bytes 221188
  18.6 1.7 copy-start.2
  23.0 2.8 %copy-start.3 = (s32[1,7]{1,0:T(1,128)S(1)}, s32[1,7]{1,0:T(1,128)}, u32[]{:S(2)}) copy-start(s32[1,7]{1,0:T(1,128)} %param.20) | copy-start | bytes 88
  88.8 31.9 %copy-start = (f32[7168]{0:T(1024)S(1)}, f32[7168]{0:T(1024)}, u32[]{:S(2)}) copy-start(f32[7168]{0:T(1024)} %param.24) | copy-start | bytes 86020
